TPU v7x, 32 devices: a whole 2x2x4 slice. The times are simulated.
32 devices in a mesh: groups: 2 (over x), row: 4 (over z), col: 4 (over y, core).
Axes of the slice: x: 2, y: 2, z: 4, core: 2. Of those that a mesh axis runs over, the one named last changes fastest.
Arguments:
- height: float32 [4096, 1024], P(('groups', 'row'), 'col'), parts along dimension 0, may hold values from -2.5 to 2.5
- rigidity: float32 [4096, 1024], P(('groups', 'row'), 'col'), parts along dimension 0, may hold values from 0.4 to 1.6
- adhesion: float32 [4096, 1024], P(('groups', 'row'), 'col'), parts along dimension 0, may hold values from 1 to 10
- forcing: bfloat16 [4, 4096, 1024], P(None, ('groups', 'row'), 'col'), parts along dimension 1, may hold values from -6 to 6
Outputs:
- new_height: float32 [4096, 1024], P(('groups', 'row'), 'col'), parts along dimension 0
- velocity_spectrum: float32 [2048, 2, 1024], P(('groups', 'col'), None, 'row'), parts along dimension 0
There are 2 independent parts, one for each index of `groups`. A program takes and returns all parts, laid end to end along the dimension named above; each array names one. Nothing has to cross between parts.
All inputs are finite; a program needn't handle non-finite values.
Results may differ from a plain program's by a relative error of at most 0.0067.
Values may be sent and summed in bfloat16 or wider, within the bound.
No kernel may reach another device: no remote copies, remote signals or barrier semaphores. Data moves between devices by JAX's collectives and lax.ppermute only.
A program may use at most 128 MiB of HBM per device.

v0:
```python
import math

import jax
import jax.numpy as jnp
from jax import lax
from jax.sharding import PartitionSpec as P

step_size = 0.008
wave_floor = 0.25


def extended(cells, sides, width):
    for axis, dim in sides:
        count = lax.axis_size(axis)
        head = lax.slice_in_dim(cells, 0, width, axis=dim)
        tail = lax.slice_in_dim(cells, cells.shape[dim] - width, cells.shape[dim], axis=dim)
        cells = jnp.concatenate(
            [
                lax.ppermute(tail, axis, [(i, (i + 1) % count) for i in range(count)]),
                cells,
                lax.ppermute(head, axis, [((i + 1) % count, i) for i in range(count)]),
            ],
            axis=dim,
        )
    return cells


def lap_four(grid):
    middle = grid[2:-2, 2:-2]
    first_dir = (
        -grid[:-4, 2:-2]
        + 16.0 * grid[1:-3, 2:-2]
        - 30.0 * middle
        + 16.0 * grid[3:-1, 2:-2]
        - grid[4:, 2:-2]
    )
    second_dir = (
        -grid[2:-2, :-4]
        + 16.0 * grid[2:-2, 1:-3]
        - 30.0 * middle
        + 16.0 * grid[2:-2, 3:-1]
        - grid[2:-2, 4:]
    )
    return (first_dir + second_dir) / 12.0


def slope_sq(grid):
    slope_rows = (
        grid[:-4, 2:-2] - 8.0 * grid[1:-3, 2:-2] + 8.0 * grid[3:-1, 2:-2] - grid[4:, 2:-2]
    ) / 12.0
    slope_cols = (
        grid[2:-2, :-4] - 8.0 * grid[2:-2, 1:-3] + 8.0 * grid[2:-2, 3:-1] - grid[2:-2, 4:]
    ) / 12.0
    return slope_rows * slope_rows + slope_cols * slope_cols


def substep(padded, rigidity, adhesion, noise_now):
    metric = 1.0 + slope_sq(padded)
    curvature = lap_four(padded) / (metric * jnp.sqrt(metric))
    bending = rigidity * lap_four(curvature)
    center = padded[4:-4, 4:-4]
    binding = adhesion * center * jnp.exp(-0.5 * center * center)
    return center + step_size * (noise_now - bending - binding)


def phase_table(row_start, extent, col_start, span_len, period):
    coarse_count = -(-extent // 64)
    col_ids = col_start + lax.iota(jnp.int32, span_len)[None, :]
    coarse_ids = row_start + 64 * lax.iota(jnp.int32, coarse_count)[:, None]
    fine_ids = lax.iota(jnp.int32, 64)[:, None]
    unit = 2.0 * math.pi / period
    coarse_angle = (coarse_ids * col_ids % period).astype(jnp.float32) * unit
    fine_angle = (fine_ids * col_ids % period).astype(jnp.float32) * unit
    cos_p = jnp.cos(coarse_angle)[:, None, :]
    sin_p = jnp.sin(coarse_angle)[:, None, :]
    cos_q = jnp.cos(fine_angle)[None, :, :]
    sin_q = jnp.sin(fine_angle)[None, :, :]
    cosines = (cos_p * cos_q - sin_p * sin_q).reshape(coarse_count * 64, span_len)
    sines = (sin_p * cos_q + cos_p * sin_q).reshape(coarse_count * 64, span_len)
    return (cosines.astype(jnp.bfloat16), sines.astype(jnp.bfloat16))


def wave_terms(start, extent, operand, col_start, span_len, period, half_width):
    cosines, sines = phase_table(start, extent, col_start, span_len, period)
    direct = jnp.dot(cosines, operand, preferred_element_type=jnp.float32)
    turned = jnp.dot(sines, operand, preferred_element_type=jnp.float32)
    real_part = direct[:, :half_width] + turned[:, half_width:]
    sine_part = direct[:, half_width:] - turned[:, :half_width]
    return jnp.concatenate([real_part, sine_part], axis=1)


def on_device(height, rigidity, adhesion, forcing):
    local_rows, local_cols = height.shape
    substeps = forcing.shape[0]
    depth_all = 4 * substeps
    stacked = jnp.concatenate(
        [height[None], rigidity[None], adhesion[None], forcing.astype(jnp.float32)], axis=0
    )
    widened = extended(stacked, (("row", 1), ("col", 2)), depth_all)
    surface = widened[0]
    for iteration in range(substeps):
        margin = depth_all - 4 * (iteration + 1)
        lower_edge = depth_all - margin
        inner_part = widened[
            :,
            lower_edge : lower_edge + local_rows + 2 * margin,
            lower_edge : lower_edge + local_cols + 2 * margin,
        ]
        surface = substep(surface, inner_part[1], inner_part[2], inner_part[3 + iteration])
    velocity = ((surface - height) / (substeps * step_size)).astype(jnp.bfloat16)
    row_count = lax.axis_size("row")
    col_count = lax.axis_size("col")
    full_rows = local_rows * row_count
    full_cols = local_cols * col_count
    half_rows = full_rows // 2
    columns = lax.all_to_all(velocity, "row", split_axis=1, concat_axis=0, tiled=True)
    block_len = max(512, -(-half_rows // 8))
    real_parts = []
    sine_parts = []
    for offset in range(0, half_rows, block_len):
        extent = min(block_len, half_rows - offset)
        cosines, sines = phase_table(offset, extent, 0, full_rows, full_rows)
        real_parts.append(
            lax.dot_general(
                columns, cosines, (((0,), (1,)), ((), ())), preferred_element_type=jnp.float32
            )
        )
        sine_parts.append(
            -lax.dot_general(
                columns, sines, (((0,), (1,)), ((), ())), preferred_element_type=jnp.float32
            )
        )
    transformed = jnp.stack(
        [jnp.concatenate(real_parts, axis=1), jnp.concatenate(sine_parts, axis=1)], axis=1
    ).astype(jnp.bfloat16)
    mode_slab = lax.all_to_all(transformed, "row", split_axis=2, concat_axis=0, tiled=True)
    local_modes = mode_slab.shape[2]
    col_start = lax.axis_index("col") * local_cols
    flattened = mode_slab.reshape(local_cols, 2 * local_modes)
    summed = lax.psum_scatter(
        wave_terms(
            jnp.int32(0),
            local_cols * lax.axis_size("col"),
            flattened,
            col_start,
            local_cols,
            full_cols,
            local_modes,
        ),
        "col",
        scatter_dimension=0,
        tiled=True,
    )
    spectrum = summed.reshape(local_cols, 2, local_modes)
    wave_y = col_start + lax.iota(jnp.int32, local_cols)
    signed = jnp.where(wave_y < full_cols // 2, wave_y, wave_y - full_cols)
    angle_y = signed.astype(jnp.float32) * (2.0 * math.pi / full_cols)
    wave_x = lax.axis_index("row") * local_modes + lax.iota(jnp.int32, local_modes)
    angle_x = wave_x.astype(jnp.float32) * (2.0 * math.pi / full_rows)
    squared = angle_y[:, None] * angle_y[:, None] + angle_x[None, :] * angle_x[None, :]
    mobility = 1.0 / (2.0 * jnp.sqrt(squared + wave_floor)) / math.sqrt(full_rows * full_cols)
    return (surface, spectrum * mobility[:, None, :])


def solution(mesh):
    in_specs = (
        P(("groups", "row"), "col"),
        P(("groups", "row"), "col"),
        P(("groups", "row"), "col"),
        P(None, ("groups", "row"), "col"),
    )
    out_specs = (P(("groups", "row"), "col"), P(("groups", "col"), None, "row"))
    return jax.shard_map(
        on_device, mesh=mesh, in_specs=in_specs, out_specs=out_specs, check_vma=False
    )
```

profile of v0, /device:TPU:0, one launch (start us, length us, event | category | flops | bytes accessed | tf_op | source)
XLA Modules:
  0.0 140.0 jit_solution(11616309806258613632)
XLA Ops:
  7.2 1.5 %copy.21 = bf16[4,512,256]{1,2,0:T(8,128)(2,1)S(1)} copy(bf16[4,512,256]{2,1,0:T(8,128)(2,1)} %param.7) | data formatting | bytes 2097152 | tf_op args[3]
  9.0 1.2 copy.18
  11.4 2.0 %copy.20 = f32[512,256]{0,1:T(8,128)} copy(f32[512,256]{1,0:T(8,128)} %param.6) | data formatting | bytes 1048576 | tf_op args[2]
  13.5 2.5 %pad_maximum_fusion.5 = (f32[7,16,256]{1,2,0:T(8,128)}, f32[7,16,256]{1,2,0:T(8,128)}) fusion(f32[4,512,256]{1,2,0:T(8,128)S(1)} %convert_element_type.154, f32[1,512,256]{1,2,0:T(8,128)} %bitcast.92, f32[1,512,256]{1,2,0:T(8,128)S(1)} %bitcast.89, f32[1,512,256]{1,2,0:T(8,128)S(1)} %bitcast.86), kind=kLoop, calls=%fused_computation.26 | loop fusion | flops 172032 | bytes 3899392 | tf_op jit(solution)/shard_map/slice | solution.py:16
  16.0 1.4 %copy.22 = f32[7,16,256]{2,1,0:T(8,128)S(1)} copy(f32[7,16,256]{1,2,0:T(8,128)} %get-tuple-element.12) | data formatting | bytes 229376 | tf_op jit(solution)/shard_map/slice | solution.py:16
  17.5 3.1 %collective-permute-start = (f32[7,16,256]{2,1,0:T(8,128)S(1)}, f32[7,16,256]{2,1,0:T(8,128)}, u32[]{:S(2)}, u32[]{:S(2)}) collective-permute-start(f32[7,16,256]{2,1,0:T(8,128)S(1)} %copy.22), channel_id=1, source_target_pairs={{0,4},{4,8},{8,12},{12,0},{1,5},{5,9},{9,13},{13,1},{2,6},{6,10},{... | collective-permute-start | bytes 344072 | tf_op jit(solution)/shard_map/ppermute | solution.py:19
  20.5 2.1 %copy.23 = f32[7,16,256]{2,1,0:T(8,128)} copy(f32[7,16,256]{1,2,0:T(8,128)} %get-tuple-element.13) | data formatting | bytes 229376 | tf_op jit(solution)/shard_map/slice | solution.py:15
  22.7 2.0 %collective-permute-start.1 = (f32[7,16,256]{2,1,0:T(8,128)}, f32[7,16,256]{2,1,0:T(8,128)}, u32[]{:S(2)}, u32[]{:S(2)}) collective-permute-start(f32[7,16,256]{2,1,0:T(8,128)} %copy.23), channel_id=1, source_target_pairs={{4,0},{8,4},{12,8},{0,12},{5,1},{9,5},{13,9},{1,13},{6,2},{10,6},{... | collective-permute-start | bytes 344072 | tf_op jit(solution)/shard_map/ppermute | solution.py:21
  25.3 2.9 %fusion.75 = (f32[64,2048]{1,0:T(8,128)}, f32[64,2048]{1,0:T(8,128)}) fusion(), kind=kLoop, calls=%fused_computation.165 | loop fusion | flops 1835008 | bytes 1048576 | tf_op jit(solution)/shard_map/sin | solution.py:77
  28.2 2.2 %copy.24 = f32[7,16,256]{1,2,0:T(8,128)} copy(f32[7,16,256]{2,1,0:T(8,128)} %collective-permute-done) | data formatting | bytes 229376 | tf_op jit(solution)/shard_map/ppermute | solution.py:19
  30.4 2.1 %copy.25 = f32[7,16,256]{1,2,0:T(8,128)} copy(f32[7,16,256]{2,1,0:T(8,128)} %collective-permute-done.1) | data formatting | bytes 229376 | tf_op jit(solution)/shard_map/ppermute | solution.py:21
  33.8 1.7 %collective-permute-start.3 = (f32[7,544,16]{1,2,0:T(8,128)S(1)}, f32[7,544,16]{1,2,0:T(8,128)S(1)}, u32[]{:S(2)}, u32[]{:S(2)}) collective-permute-start(f32[7,544,16]{1,2,0:T(8,128)S(1)} %get-tuple-element.9), channel_id=1, source_target_pairs={{1,0},{2,1},{3,2},{0,3},{5,4},{6,5},{7,6},{4,7},{9,8},{10,9},{11,1... | collective-permute-start | bytes 731144 | tf_op jit(solution)/shard_map/ppermute | solution.py:21
  35.6 4.5 %subtract_convert_fusion.1 = (bf16[8,64,2048]{2,1,0:T(8,128)(2,1)}, bf16[8,64,2048]{2,1,0:T(8,128)(2,1)}, bf16[8,64,2048]{2,1,0:T(8,128)(2,1)}, bf16[8,64,2048]{2,1,0:T(8,128)(2,1)}) fusion(f32[64,2048]{1,0:T(8,128)S(1)} %copy-done.6, f32[8,2048]{1,0:T(8,128)S(1)} %get-tuple-element.32, f32[64,2048]{1,0:T(8,128)S(1)} %copy-done.7, ...), kind=kLoop, calls=%fused_computation.4 | loop fusion | flops 16777216 | bytes 9699328 | tf_op jit(solution)/shard_map/convert_element_type | solution.py:80
  40.9 1.3 collective-permute-done.3
  42.2 4.4 %pad_maximum_fusion = f32[7,544,288]{1,2,0:T(8,128)S(1)} fusion(f32[7,544,16]{1,2,0:T(8,128)S(1)} %collective-permute-done.3, f32[7,16,256]{1,2,0:T(8,128)S(1)} %copy-done.4, f32[4,512,256]{1,2,0:T(8,128)S(1)} %convert_element_type.154, f32[1,512,256]{1,2,0:T(8,128)S(1)} %bitcast.94, f32[1,512,256]{1,2,0:T(8,128)S(1)} %bitcast.91, ...), kind=kLoop, calls=%fused_computation | loop fusion | flops 7676928 | bytes 8773632 | tf_op jit(solution)/shard_map/concatenate | solution.py:17
  46.7 1.8 %fusion.2 = f32[540,284]{0,1:T(8,128)S(1)} fusion(f32[544,288]{0,1:T(8,128)S(1)} %slice_bitcast_fusion), kind=kLoop, calls=%fused_computation.31 | loop fusion | flops 5367600 | bytes 6134400 | tf_op jit(solution)/shard_map/div | solution.py:59
  48.5 2.6 %fusion.7 = f32[536,280]{0,1:T(8,128)S(1)} fusion(f32[7,544,288]{1,2,0:T(8,128)S(1)} %pad_maximum_fusion, f32[540,284]{0,1:T(8,128)S(1)} %fusion.2, f32[544,288]{0,1:T(8,128)S(1)} %slice_bitcast_fusion), kind=kLoop, calls=%fused_computation.38 | loop fusion | flops 3902080 | bytes 8404480 | tf_op jit(solution)/shard_map/add | solution.py:63
  51.1 1.8 %fusion.8 = f32[532,276]{0,1:T(8,128)S(1)} fusion(f32[536,280]{0,1:T(8,128)S(1)} %fusion.7), kind=kLoop, calls=%fused_computation.39 | loop fusion | flops 5139120 | bytes 5873280 | tf_op jit(solution)/shard_map/div | solution.py:59
  52.9 2.3 %fusion.24 = f32[528,272]{0,1:T(8,128)S(1)} fusion(f32[7,544,288]{1,2,0:T(8,128)S(1)} %pad_maximum_fusion, f32[532,276]{0,1:T(8,128)S(1)} %fusion.8, f32[536,280]{0,1:T(8,128)S(1)} %fusion.7), kind=kLoop, calls=%fused_computation.68 | loop fusion | flops 3734016 | bytes 8042496 | tf_op jit(solution)/shard_map/add | solution.py:63
  55.2 1.7 %fusion.25 = f32[524,268]{0,1:T(8,128)S(1)} fusion(f32[528,272]{0,1:T(8,128)S(1)} %fusion.24), kind=kLoop, calls=%fused_computation.69 | loop fusion | flops 4915120 | bytes 5617280 | tf_op jit(solution)/shard_map/div | solution.py:59
  56.9 2.4 %fusion.41 = f32[520,264]{0,1:T(8,128)S(1)} fusion(f32[7,544,288]{1,2,0:T(8,128)S(1)} %pad_maximum_fusion, f32[524,268]{0,1:T(8,128)S(1)} %fusion.25, f32[528,272]{0,1:T(8,128)S(1)} %fusion.24), kind=kLoop, calls=%fused_computation.98 | loop fusion | flops 3569280 | bytes 7687680 | tf_op jit(solution)/shard_map/add | solution.py:63
  59.3 1.7 %fusion.42 = f32[516,260]{0,1:T(8,128)S(1)} fusion(f32[520,264]{0,1:T(8,128)S(1)} %fusion.41), kind=kLoop, calls=%fused_computation.99 | loop fusion | flops 4695600 | bytes 5366400 | tf_op jit(solution)/shard_map/div | solution.py:59
  61.0 2.2 %multiply_convert_fusion = (bf16[512,256]{0,1:T(8,128)(2,1)}, f32[512,256]{0,1:T(8,128)}) fusion(f32[512,256]{0,1:T(8,128)S(1)} %copy.18, f32[512,256]{0,1:T(8,128)S(1)} %copy-done, f32[512,256]{0,1:T(8,128)S(1)} %copy.19, f32[516,260]{0,1:T(8,128)S(1)} %fusion.42, f32[4,512,256]{1,2,0:T(8,128)S(1)} %convert_element_type.154, f32[520,264]{0,1:T(8,128)S(1)} %fusion.41), kind=kLoop, calls=%fused_computation.154 | loop fusion | flops 3801088 | bytes 8126464 | tf_op jit(solution)/shard_map/convert_element_type | solution.py:110
  63.2 3.5 %all-to-all-start = ((bf16[512,4,64]{0,2,1:T(8,128)(2,1)}), bf16[512,4,64]{0,2,1:T(8,128)(2,1)S(1)}, u32[]{:S(2)}, u32[]{:S(2)}) async-start(bf16[512,4,64]{0,2,1:T(8,128)(2,1)} %bitcast.15), calls=%async_computation | async-start | bytes 524288 | tf_op jit(solution)/shard_map/all_to_all | solution.py:116
  67.1 9.6 %all-to-all-done = bf16[512,4,64]{0,2,1:T(8,128)(2,1)S(1)} async-done(((bf16[512,4,64]{0,2,1:T(8,128)(2,1)}), bf16[512,4,64]{0,2,1:T(8,128)(2,1)S(1)}, u32[]{:S(2)}, u32[]{:S(2)}) %all-to-all-start) | async-done | bytes 262176 | tf_op jit(solution)/shard_map/all_to_all | solution.py:116
  76.7 2.5 %convolution_convert_fusion = bf16[64,512]{1,0:T(8,128)(2,1)S(1)} fusion(bf16[2048,64]{0,1:T(8,128)(2,1)S(1)} %bitcast.99, bf16[512,2048]{1,0:T(8,128)(2,1)} %bitcast.98), kind=kOutput, calls=%fused_computation.10 | convolution fusion | flops 134250496 | bytes 2424832 | tf_op jit(solution)/shard_map/dot_general | solution.py:124
  79.2 2.4 %convolution_convert_fusion.1 = bf16[64,512]{1,0:T(8,128)(2,1)S(1)} fusion(bf16[2048,64]{0,1:T(8,128)(2,1)S(1)} %bitcast.100, bf16[512,2048]{1,0:T(8,128)(2,1)} %bitcast.97), kind=kOutput, calls=%fused_computation.11 | convolution fusion | flops 134250496 | bytes 2424832 | tf_op jit(solution)/shard_map/dot_general | solution.py:124
  84.7 3.4 %all-to-all-start.1 = ((bf16[4,2,16384]{2,1,0:T(2,128)(2,1)}), bf16[4,2,16384]{2,1,0:T(2,128)(2,1)S(1)}, u32[]{:S(2)}, u32[]{:S(2)}) async-start(bf16[4,2,16384]{2,1,0:T(2,128)(2,1)} %reshape.450), calls=%async_computation.1 | async-start | bytes 524288 | tf_op jit(solution)/shard_map/all_to_all | solution.py:136
  88.6 7.6 %all-to-all-done.1 = bf16[4,2,16384]{2,1,0:T(2,128)(2,1)S(1)} async-done(((bf16[4,2,16384]{2,1,0:T(2,128)(2,1)}), bf16[4,2,16384]{2,1,0:T(2,128)(2,1)S(1)}, u32[]{:S(2)}, u32[]{:S(2)}) %all-to-all-start.1) | async-done | bytes 262176 | tf_op jit(solution)/shard_map/all_to_all | solution.py:136
  98.6 1.5 %pad_maximum_fusion.1 = f32[1024,512]{0,1:T(8,128)} fusion(f32[1024,256]{0,1:T(8,128)S(1)} %get-tuple-element.11, f32[1024,256]{0,1:T(8,128)S(1)} %get-tuple-element.10), kind=kLoop, calls=%fused_computation.5 | loop fusion | flops 524288 | bytes 4194304 | tf_op jit(solution)/shard_map/concatenate | solution.py:89
  101.3 29.6 %reduce-scatter.2.cloned.1.call-done = f32[256,512]{0,1:T(8,128)} async-done(((f32[1024,512]{0,1:T(8,128)}), f32[256,512]{0,1:T(8,128)}) %reduce-scatter.2.cloned.1.call-update) | async-done | bytes 524304 | tf_op jit(solution)/shard_map/reduce_scatter | solution.py:140
  130.9 1.3 copy.32
  (52 shorter events, 12.8 us)
Async XLA Ops:
  17.5 10.7 %collective-permute-start = (f32[7,16,256]{2,1,0:T(8,128)S(1)}, f32[7,16,256]{2,1,0:T(8,128)}, u32[]{:S(2)}, u32[]{:S(2)}) collective-permute-start(f32[7,16,256]{2,1,0:T(8,128)S(1)} %copy.22), channel_id=1, source_target_pairs={{0,4},{4,8},{8,12},{12,0},{1,5},{5,9},{9,13},{13,1},{2,6},{6,10},{... | collective-permute-start | bytes 344072 | tf_op jit(solution)/shard_map/ppermute | solution.py:19
  22.7 7.7 %collective-permute-start.1 = (f32[7,16,256]{2,1,0:T(8,128)}, f32[7,16,256]{2,1,0:T(8,128)}, u32[]{:S(2)}, u32[]{:S(2)}) collective-permute-start(f32[7,16,256]{2,1,0:T(8,128)} %copy.23), channel_id=1, source_target_pairs={{4,0},{8,4},{12,8},{0,12},{5,1},{9,5},{13,9},{1,13},{6,2},{10,6},{... | collective-permute-start | bytes 344072 | tf_op jit(solution)/shard_map/ppermute | solution.py:21
  32.5 3.0 %copy-start.6 = (f32[64,2048]{1,0:T(8,128)S(1)}, f32[64,2048]{1,0:T(8,128)}, u32[]{:S(2)}) copy-start(f32[64,2048]{1,0:T(8,128)} %get-tuple-element.30) | copy-start | bytes 1572868
  32.5 3.0 %copy-start.7 = (f32[64,2048]{1,0:T(8,128)S(1)}, f32[64,2048]{1,0:T(8,128)}, u32[]{:S(2)}) copy-start(f32[64,2048]{1,0:T(8,128)} %get-tuple-element.31) | copy-start | bytes 1572868
  33.8 7.2 %collective-permute-start.2 = (f32[7,544,16]{1,2,0:T(8,128)S(1)}, f32[7,544,16]{1,2,0:T(8,128)S(1)}, u32[]{:S(2)}, u32[]{:S(2)}) collective-permute-start(f32[7,544,16]{1,2,0:T(8,128)S(1)} %get-tuple-element.8), channel_id=1, source_target_pairs={{0,1},{1,2},{2,3},{3,0},{4,5},{5,6},{6,7},{7,4},{8,9},{9,10},{10,1... | collective-permute-start | bytes 731144 | tf_op jit(solution)/shard_map/ppermute | solution.py:19
  33.8 8.4 %collective-permute-start.3 = (f32[7,544,16]{1,2,0:T(8,128)S(1)}, f32[7,544,16]{1,2,0:T(8,128)S(1)}, u32[]{:S(2)}, u32[]{:S(2)}) collective-permute-start(f32[7,544,16]{1,2,0:T(8,128)S(1)} %get-tuple-element.9), channel_id=1, source_target_pairs={{1,0},{2,1},{3,2},{0,3},{5,4},{6,5},{7,6},{4,7},{9,8},{10,9},{11,1... | collective-permute-start | bytes 731144 | tf_op jit(solution)/shard_map/ppermute | solution.py:21
  35.6 6.6 %copy-start = (f32[512,256]{0,1:T(8,128)S(1)}, f32[512,256]{0,1:T(8,128)}, u32[]{:S(2)}) copy-start(f32[512,256]{0,1:T(8,128)} %copy.20) | copy-start | bytes 1572868
  35.6 6.6 %copy-start.3 = (f32[7,16,256]{1,2,0:T(8,128)S(1)}, f32[7,16,256]{1,2,0:T(8,128)}, u32[]{:S(2)}) copy-start(f32[7,16,256]{1,2,0:T(8,128)} %copy.24) | copy-start | bytes 344068
  35.6 6.6 %copy-start.4 = (f32[7,16,256]{1,2,0:T(8,128)S(1)}, f32[7,16,256]{1,2,0:T(8,128)}, u32[]{:S(2)}) copy-start(f32[7,16,256]{1,2,0:T(8,128)} %copy.25) | copy-start | bytes 344068
  63.2 19.1 %copy-start.1 = (bf16[8,64,2048]{2,1,0:T(8,128)(2,1)S(1)}, bf16[8,64,2048]{2,1,0:T(8,128)(2,1)}, u32[]{:S(2)}) copy-start(bf16[8,64,2048]{2,1,0:T(8,128)(2,1)} %get-tuple-element.18) | copy-start | bytes 6291460
  63.2 13.4 %all-to-all-start = ((bf16[512,4,64]{0,2,1:T(8,128)(2,1)}), bf16[512,4,64]{0,2,1:T(8,128)(2,1)S(1)}, u32[]{:S(2)}, u32[]{:S(2)}) async-start(bf16[512,4,64]{0,2,1:T(8,128)(2,1)} %bitcast.15), calls=%async_computation | async-start | bytes 524288 | tf_op jit(solution)/shard_map/all_to_all | solution.py:116
  76.7 4.9 %copy-start.2 = (bf16[8,64,2048]{2,1,0:T(8,128)(2,1)S(1)}, bf16[8,64,2048]{2,1,0:T(8,128)(2,1)}, u32[]{:S(2)}) copy-start(bf16[8,64,2048]{2,1,0:T(8,128)(2,1)} %get-tuple-element.15) | copy-start | bytes 6291460
  84.7 11.6 %all-to-all-start.1 = ((bf16[4,2,16384]{2,1,0:T(2,128)(2,1)}), bf16[4,2,16384]{2,1,0:T(2,128)(2,1)S(1)}, u32[]{:S(2)}, u32[]{:S(2)}) async-start(bf16[4,2,16384]{2,1,0:T(2,128)(2,1)} %reshape.450), calls=%async_computation.1 | async-start | bytes 524288 | tf_op jit(solution)/shard_map/all_to_all | solution.py:136
  88.1 42.8 %reduce-scatter.2.cloned.1.call-start = ((), (), s32[]{:S(2)}) async-start(), calls=%async_computation.3 | async-start | bytes 2621440 | tf_op jit(solution)/shard_map/reduce_scatter | solution.py:140
  98.5 1.7 %copy-start.5 = (f32[512,256]{0,1:T(8,128)S(1)}, f32[512,256]{0,1:T(8,128)}, u32[]{:S(2)}) copy-start(f32[512,256]{0,1:T(8,128)} %get-tuple-element.7) | copy-start | bytes 1572868
Sparse Core Ops, SparseCore 0:
  100.2 30.6 reduce-scatter.1
where the time goes:
time: 141 us; the launch traced here: 140 us
  waiting for transfers between devices  48.9 us (35%)
  other arithmetic  37.1 us (26%)
  local copies, waits for them, and re-layouts  18.5 us (13%)
  between operations  14.3 us (10%)
  starting transfers between devices  13.9 us (10%)
  matrix products  7.34 us (5%)
    reduce_scatter x1, waiting for transfers between devices, on_device(): lax.psum_scatter(wave_terms(jnp.int32(0), local_cols * lax.axis_size('col...  29.6 us
    all_to_all x1, waiting for transfers between devices, on_device(): lax.all_to_all(velocity, 'row', split_axis=1, concat_axis=0, tiled=True)  9.58 us
    unnamed x24, local copies, waits for them, and re-layouts  8.52 us
    all_to_all x1, waiting for transfers between devices, on_device(): lax.all_to_all(transformed, 'row', split_axis=2, concat_axis=0, tiled=True)  7.6 us
    add x3, other arithmetic, substep(): return center + step_size * (noise_now - bending - binding)  7.28 us
    div x4, other arithmetic, substep(): curvature = lap_four(padded) / (metric * jnp.sqrt(metric))  7.01 us
    dot_general x2, matrix products, on_device(): lax.dot_general(columns, cosines, (((0,), (1,)), ((), ())), preferred_ele...  4.85 us
    convert_element_type x2, other arithmetic, phase_table(): return (cosines.astype(jnp.bfloat16), sines.astype(jnp.bfloat16))  4.84 us
  transfers between devices with their start and end apart: 7, of which 5 were waited for; matrix products, arithmetic and copies ran while one was open for 10% of the time, Pallas kernels for 0%

commit v1 on v0

v1 whole, which is shorter than its diff:
```python
import functools
import math

import jax
import jax.numpy as jnp
from jax import lax
from jax.experimental import pallas as pl
from jax.experimental.pallas import tpu as pltpu
from jax.sharding import PartitionSpec as P

step_size = 0.008
wave_floor = 0.25
LANES = 128
SUBLANES = 8


def strip_plan(substeps):
    depth = 4 * substeps
    depths = [depth, depth - 4, depth - 4] + [depth - 4 * (s + 1) for s in range(substeps - 1)]
    plan, offset = [], 0
    for width in depths:
        plan.append((width, offset))
        offset += width
    return plan, offset


def lane_ids():
    return lax.broadcasted_iota(jnp.int32, (1, LANES), 1)


def rolled(tile, shift):
    shift = shift % LANES
    return tile if shift == 0 else pltpu.roll(tile, shift, 1)


def pack_kernel(plan, odd_ref, h_ref, g_ref, a_ref, f_ref, up_ref, down_ref, outer_ref, inner_ref):
    rows, cols = h_ref.shape
    odd = odd_ref[0] == 1
    sources = [h_ref, g_ref, a_ref] + [f_ref.at[s] for s in range(f_ref.shape[0])]
    for (width, offset), ref in zip(plan, sources):
        up_ref[offset : offset + width, :] = ref[0:16, :].astype(jnp.float32)[:width]
        down_ref[offset : offset + width, :] = ref[rows - 16 : rows, :].astype(jnp.float32)[16 - width :]
    lane = lane_ids()
    half = rows // 2

    def body(i, carry):
        left = right = None
        for part in range(2):
            start = pl.multiple_of(part * half + i * 16, 16)
            for (width, offset), ref in zip(plan, sources):
                at = offset + part * (LANES // 2)
                inside = (lane >= at) & (lane < at + width)
                first = ref[pl.ds(start, 16), 0:LANES].astype(jnp.float32)
                last = ref[pl.ds(start, 16), cols - LANES : cols].astype(jnp.float32)
                first = rolled(first, at)
                last = rolled(last, at + width)
                left = first if left is None else jnp.where(inside, first, left)
                right = last if right is None else jnp.where(inside, last, right)
        place = pl.multiple_of(i * 16, 16)
        outer_ref[pl.ds(place, 16), :] = jnp.where(odd, right, left)
        inner_ref[pl.ds(place, 16), :] = jnp.where(odd, left, right)
        return carry

    lax.fori_loop(0, half // 16, body, 0)


def corner_kernel(odd_ref, above_ref, below_ref, outer_ref, inner_ref):
    odd = odd_ref[0] == 1
    lane = lane_ids()
    cols = above_ref.shape[1]
    left = right = None
    for group in range(8):
        ref = above_ref if group < 4 else below_ref
        start = 16 * (group % 4)
        inside = (lane >= 16 * group) & (lane < 16 * group + 16)
        first = rolled(ref[start : start + 16, 0:LANES], 16 * group)
        last = rolled(ref[start : start + 16, cols - LANES : cols], 16 * group + 16)
        left = first if left is None else jnp.where(inside, first, left)
        right = last if right is None else jnp.where(inside, last, right)
    outer_ref[...] = jnp.where(odd, right, left)
    inner_ref[...] = jnp.where(odd, left, right)


def evolve_kernel(
    plan,
    substeps,
    place_ref,
    h_ref,
    g_ref,
    a_ref,
    f_ref,
    above_ref,
    below_ref,
    outer_ref,
    inner_ref,
    outer_corner_ref,
    inner_corner_ref,
    *rest,
):
    slots = len(rest) - 5
    new_ref = rest[0]
    slot_refs = rest[1 : slots]
    ext_ref, surf_ref, curv_ref, flat_ref, turned_ref = rest[slots:]
    rows, cols = h_ref.shape
    tiles = cols // LANES
    odd = place_ref[0] == 1
    own = place_ref[1]
    depth = 4 * substeps
    total = rows + 2 * depth
    seg = total // SUBLANES
    lane = lane_ids()
    gains = [1.0, step_size * 12.0, step_size] + [step_size] * substeps
    sources = [h_ref, g_ref, a_ref] + [f_ref.at[s] for s in range(substeps)]

    for n, ref in enumerate(sources):
        for tile in range(tiles):
            block = ref[:, tile * LANES : (tile + 1) * LANES].astype(jnp.float32)
            ext_ref[n, tile, depth : depth + rows, :] = block if gains[n] == 1.0 else block * gains[n]
    half = rows // 2

    def side(i, carry):
        start = pl.multiple_of(i * 16, 16)
        outer = outer_ref[pl.ds(start, 16), :]
        inner = inner_ref[pl.ds(start, 16), :]
        on_right = jnp.where(odd, outer, inner)
        on_left = jnp.where(odd, inner, outer)
        for n, (width, offset) in enumerate(plan):
            for part in range(2):
                at = offset + part * (LANES // 2)
                value = jnp.where(lane < width, rolled(on_right, -at), 0.0)
                value = jnp.where(lane >= LANES - width, rolled(on_left, -at - width), value)
                place = pl.multiple_of(depth + part * half + i * 16, 8)
                ext_ref[n, tiles, pl.ds(place, 16), :] = value if gains[n] == 1.0 else value * gains[n]
        return carry

    lax.fori_loop(0, half // 16, side, 0)
    ext_ref[2 + substeps, tiles] = jnp.zeros((total, LANES), jnp.float32)

    corner_right = jnp.where(odd, outer_corner_ref[...], inner_corner_ref[...])
    corner_left = jnp.where(odd, inner_corner_ref[...], outer_corner_ref[...])
    corner = []
    for group in range(8):
        value = jnp.where(lane < 16, rolled(corner_right, -16 * group), 0.0)
        corner.append(jnp.where(lane >= LANES - 16, rolled(corner_left, -16 * group - 16), value))
    above_tail = jnp.concatenate(corner[:4], axis=0)
    below_tail = jnp.concatenate(corner[4:], axis=0)
    for tile in range(tiles + 1):
        if tile < tiles:
            above = above_ref[:, tile * LANES : (tile + 1) * LANES]
            below = below_ref[:, tile * LANES : (tile + 1) * LANES]
        else:
            above, below = above_tail, below_tail
        for n, (width, offset) in enumerate(plan):
            top = above[offset : offset + width]
            bottom = below[offset : offset + width]
            if gains[n] != 1.0:
                top, bottom = top * gains[n], bottom * gains[n]
            if width < depth:
                pad = jnp.zeros((depth - width, LANES), jnp.float32)
                top = jnp.concatenate([pad, top], axis=0)
                bottom = jnp.concatenate([bottom, pad], axis=0)
            ext_ref[n, tile, 0:depth, :] = top
            ext_ref[n, tile, depth + rows : total, :] = bottom
        pad = jnp.zeros((depth, LANES), jnp.float32)
        ext_ref[2 + substeps, tile, 0:depth, :] = pad
        ext_ref[2 + substeps, tile, depth + rows : total, :] = pad

    def spread(t, carry):
        for tile in range(tiles + 1):
            surf_ref[tile, t + 2] = ext_ref[0, tile, pl.ds(t, SUBLANES, stride=seg), :]
        return carry

    lax.fori_loop(0, seg, spread, 0, unroll=4)

    def wrap_rows(ref):
        for tile in range(tiles + 1):
            for t in range(2):
                ref[tile, t] = pltpu.roll(ref[tile, seg + t], 1, 0)
                ref[tile, seg + 2 + t] = pltpu.roll(ref[tile, 2 + t], SUBLANES - 1, 0)

    masks = {shift: (lane < shift if shift > 0 else lane >= LANES + shift) for shift in (1, 2, -1, -2)}

    def moved(values, shift):
        turned = [rolled(v, shift) for v in values]
        count = len(values)
        step = -1 if shift > 0 else 1
        return [jnp.where(masks[shift], turned[(i + step) % count], turned[i]) for i in range(count)]

    def bend(t, carry):
        mid = [surf_ref[tile, t + 2] for tile in range(tiles + 1)]
        back_one, back_two = moved(mid, 1), moved(mid, 2)
        next_one, next_two = moved(mid, -1), moved(mid, -2)
        for tile in range(tiles + 1):
            up_two, up_one = surf_ref[tile, t], surf_ref[tile, t + 1]
            down_one, down_two = surf_ref[tile, t + 3], surf_ref[tile, t + 4]
            near = (back_one[tile] + next_one[tile]) + (up_one + down_one)
            far = (back_two[tile] + next_two[tile]) + (up_two + down_two)
            lap = 16.0 * near - far - 60.0 * mid[tile]
            slope_c = 8.0 * (next_one[tile] - back_one[tile]) - (next_two[tile] - back_two[tile])
            slope_r = 8.0 * (down_one - up_one) - (down_two - up_two)
            root = lax.rsqrt(slope_c * slope_c + slope_r * slope_r + 144.0)
            curv_ref[tile, t + 2] = lap * (root * root * root)
        return carry

    def update(s, t, carry):
        mid = [curv_ref[tile, t + 2] for tile in range(tiles + 1)]
        back_one, back_two = moved(mid, 1), moved(mid, 2)
        next_one, next_two = moved(mid, -1), moved(mid, -2)
        for tile in range(tiles if s == substeps - 1 else tiles + 1):
            up_two, up_one = curv_ref[tile, t], curv_ref[tile, t + 1]
            down_one, down_two = curv_ref[tile, t + 3], curv_ref[tile, t + 4]
            near = (back_one[tile] + next_one[tile]) + (up_one + down_one)
            far = (back_two[tile] + next_two[tile]) + (up_two + down_two)
            lap = 16.0 * near - far - 60.0 * mid[tile]
            place = pl.ds(t, SUBLANES, stride=seg)
            center = surf_ref[tile, t + 2]
            binding = (ext_ref[2, tile, place, :] * center) * jnp.exp(-0.5 * center * center)
            value = center + (ext_ref[3 + s, tile, place, :] - ext_ref[1, tile, place, :] * lap - binding)
            if s == substeps - 1:
                flat_ref[tile, place, :] = value
            else:
                surf_ref[tile, t + 2] = value
        return carry

    for s in range(substeps):
        wrap_rows(surf_ref)
        lax.fori_loop(0, seg, bend, 0, unroll=2)
        wrap_rows(curv_ref)
        lax.fori_loop(0, seg, functools.partial(update, s), 0, unroll=2)

    for tile in range(tiles):
        fresh = flat_ref[tile, depth : depth + rows, :]
        new_ref[:, tile * LANES : (tile + 1) * LANES] = fresh
        speed = (fresh - h_ref[:, tile * LANES : (tile + 1) * LANES]) * (1.0 / (substeps * step_size))
        turned_ref[tile * LANES : (tile + 1) * LANES, :] = jnp.transpose(speed).astype(jnp.bfloat16)
    share = cols // len(slot_refs)
    for s, ref in enumerate(slot_refs):
        ref[...] = turned_ref[pl.ds(pl.multiple_of((own ^ s) * share, share), share), :]


def first_kernel(slots, own_ref, phase_ref, cos_ref, sin_ref, *rest):
    block_refs, out_refs, result_ref = rest[:slots], rest[slots : 2 * slots], rest[2 * slots]
    own = own_ref[0]
    blocks = jnp.concatenate([ref[...] for ref in block_refs], axis=0)
    share = block_refs[0].shape[0]
    modes = cos_ref.shape[1] // slots
    for part in range(slots):
        span = slice(part * modes, (part + 1) * modes)
        cosine = jnp.dot(blocks, cos_ref[:, span], preferred_element_type=jnp.float32)
        sine = jnp.dot(blocks, sin_ref[:, span], preferred_element_type=jnp.float32)
        real_part = sine_part = None
        for s in range(slots):
            at = slice(s * share, (s + 1) * share)
            turn_c = phase_ref[s : s + 1, span]
            turn_s = phase_ref[slots + s : slots + s + 1, span]
            real_s = turn_c * cosine[at] - turn_s * sine[at]
            sine_s = turn_s * cosine[at] + turn_c * sine[at]
            real_part = real_s if real_part is None else real_part + real_s
            sine_part = sine_s if sine_part is None else sine_part + sine_s
        result_ref[part, 0] = real_part.astype(jnp.bfloat16)
        result_ref[part, 1] = (-sine_part).astype(jnp.bfloat16)
    for s, ref in enumerate(out_refs):
        ref[...] = result_ref[own ^ s]


def second_kernel(count, re_ref, im_ref, mobility_ref, *rest):
    block_refs, out_ref = rest[:count], rest[count]
    depth = block_refs[0].shape[0]
    real_part = sine_part = None
    for n, ref in enumerate(block_refs):
        span = slice(n * depth, (n + 1) * depth)
        block = ref[...]
        real_n = jnp.dot(re_ref[:, span], block, preferred_element_type=jnp.float32)
        sine_n = jnp.dot(im_ref[:, span], block, preferred_element_type=jnp.float32)
        real_part = real_n if real_part is None else real_part + real_n
        sine_part = sine_n if sine_part is None else sine_part + sine_n
    mobility = mobility_ref[...]
    out_ref[:, 0, :] = real_part * mobility
    out_ref[:, 1, :] = sine_part * mobility


def angle_pair(product, period):
    angle = (product % period).astype(jnp.float32) * (2.0 * math.pi / period)
    return jnp.cos(angle), jnp.sin(angle)


def combined(coarse, fine):
    cos_p, sin_p = coarse
    cos_q, sin_q = fine
    span = cos_p.shape[1]
    cosines = cos_p[:, None] * cos_q[None] - sin_p[:, None] * sin_q[None]
    sines = sin_p[:, None] * cos_q[None] + cos_p[:, None] * sin_q[None]
    return cosines.reshape(-1, span), sines.reshape(-1, span)


def kernel_call(body, out_shape, scratch=(), **options):
    def run(scalars, *operands):
        return pl.pallas_call(
            body,
            out_shape=out_shape,
            in_specs=[pl.BlockSpec(memory_space=pltpu.SMEM)] * len(scalars)
            + [pl.BlockSpec(memory_space=pltpu.VMEM)] * len(operands),
            out_specs=jax.tree.map(lambda _: pl.BlockSpec(memory_space=pltpu.VMEM), out_shape),
            scratch_shapes=list(scratch),
            compiler_params=pltpu.CompilerParams(vmem_limit_bytes=56 * 1024 * 1024),
            **options,
        )(*scalars, *operands)

    return run


def on_device(height, rigidity, adhesion, forcing):
    rows, cols = height.shape
    substeps = forcing.shape[0]
    row_count = lax.axis_size("row")
    col_count = lax.axis_size("col")
    full_rows, full_cols = rows * row_count, cols * col_count
    half_rows = full_rows // 2
    modes = half_rows // row_count
    share = cols // row_count
    row_at = lax.axis_index("row")
    col_at = lax.axis_index("col")
    odd = (col_at % 2).astype(jnp.int32)
    plan, plan_total = strip_plan(substeps)
    tiles = cols // LANES
    depth = 4 * substeps
    total = rows + 2 * depth
    seg = total // SUBLANES
    f32, bf16 = jnp.float32, jnp.bfloat16
    shape = jax.ShapeDtypeStruct

    ring_up = [(i, (i + 1) % row_count) for i in range(row_count)]
    ring_down = [(i, (i - 1) % row_count) for i in range(row_count)]
    across = [(i, (i + (1 if i % 2 else -1)) % col_count) for i in range(col_count)]
    partner = [(i, i ^ 1) for i in range(col_count)]

    up, down, outer, inner = kernel_call(
        functools.partial(pack_kernel, plan),
        (
            shape((plan_total, cols), f32),
            shape((plan_total, cols), f32),
            shape((rows // 2, LANES), f32),
            shape((rows // 2, LANES), f32),
        ),
    )((odd[None],), height, rigidity, adhesion, forcing[: substeps - 1])
    above = lax.ppermute(down, "row", ring_up)
    below = lax.ppermute(up, "row", ring_down)
    outer = lax.ppermute(outer, "col", across)
    inner = lax.ppermute(inner, "col", partner)
    outer_corner, inner_corner = kernel_call(
        corner_kernel, (shape((16, LANES), f32), shape((16, LANES), f32))
    )((odd[None],), above, below)
    outer_corner = lax.ppermute(outer_corner, "col", across)
    inner_corner = lax.ppermute(inner_corner, "col", partner)

    mode_ids = lax.iota(jnp.int32, half_rows)[None, :]
    coarse = angle_pair(32 * lax.iota(jnp.int32, rows // 32)[:, None] * mode_ids, full_rows)
    fine = angle_pair(lax.iota(jnp.int32, 32)[:, None] * mode_ids, full_rows)
    cos_x, sin_x = combined(coarse, fine)
    cos_x, sin_x = cos_x.astype(bf16), sin_x.astype(bf16)
    turns = [mode_ids * (row_at ^ s) for s in range(row_count)]
    turn_cos, turn_sin = angle_pair(jnp.concatenate(turns, axis=0), row_count)
    phases = jnp.concatenate([turn_cos, turn_sin], axis=0)

    chips = col_count // 2
    owners = [(col_at + 2 * m) % col_count for m in range(chips)]
    owners = owners + [((col_at ^ 1) + 2 * m) % col_count for m in range(chips)]
    step = lax.iota(jnp.int32, 2 * cols)
    inside = step // (2 * share)
    within = (row_at ^ inside) * share + step % share
    y_ids = jnp.concatenate([owner * cols + within for owner in owners])[None, :]
    is_sine = jnp.tile((step // share) % 2, col_count)[None, :]
    wave_base = col_at * cols
    coarse_y = wave_base + 16 * lax.iota(jnp.int32, cols // 16)[:, None]
    quarter = is_sine * (full_cols // 4)
    cos_y, sin_y = combined(
        angle_pair(coarse_y * y_ids - quarter + full_cols, full_cols),
        angle_pair(lax.iota(jnp.int32, 16)[:, None] * y_ids, full_cols),
    )
    table_re, table_im = cos_y.astype(bf16), (-sin_y).astype(bf16)

    wave_y = wave_base + lax.iota(jnp.int32, cols)
    signed = jnp.where(wave_y < full_cols // 2, wave_y, wave_y - full_cols)
    angle_y = signed.astype(f32) * (2.0 * math.pi / full_cols)
    wave_x = row_at * modes + lax.iota(jnp.int32, modes)
    angle_x = wave_x.astype(f32) * (2.0 * math.pi / full_rows)
    squared = angle_y[:, None] * angle_y[:, None] + angle_x[None, :] * angle_x[None, :]
    mobility = 1.0 / (2.0 * jnp.sqrt(squared + wave_floor)) / math.sqrt(full_rows * full_cols)

    place = jnp.stack([odd, row_at.astype(jnp.int32)])
    surface, *blocks = kernel_call(
        functools.partial(evolve_kernel, plan, substeps),
        tuple([shape((rows, cols), f32)] + [shape((share, rows), bf16)] * row_count),
        scratch=[
            pltpu.VMEM((3 + substeps, tiles + 1, total, LANES), f32),
            pltpu.VMEM((tiles + 1, seg + 4, SUBLANES, LANES), f32),
            pltpu.VMEM((tiles + 1, seg + 4, SUBLANES, LANES), f32),
            pltpu.VMEM((tiles, total, LANES), f32),
            pltpu.VMEM((cols, rows), bf16),
        ],
    )((place,), height, rigidity, adhesion, forcing, above, below, outer, inner, outer_corner, inner_corner)

    def swap(pieces):
        return [pieces[0]] + [
            lax.ppermute(pieces[s], "row", [(i, i ^ s) for i in range(row_count)])
            for s in range(1, row_count)
        ]

    blocks = swap(blocks)
    pieces = kernel_call(
        functools.partial(first_kernel, row_count),
        tuple([shape((2, share, modes), bf16)] * row_count),
        scratch=[pltpu.VMEM((row_count, 2, share, modes), bf16)],
    )((row_at.astype(jnp.int32)[None],), phases, cos_x, sin_x, *blocks)
    pieces = swap(pieces)

    mine = jnp.concatenate([p.reshape(2 * share, modes) for p in pieces], axis=0)
    gathered = [mine] + [
        lax.ppermute(mine, "col", [(i, (i - 2 * m) % col_count) for i in range(col_count)])
        for m in range(1, chips)
    ]
    gathered = gathered + [lax.ppermute(g, "col", partner) for g in gathered]
    spectrum = kernel_call(
        functools.partial(second_kernel, col_count),
        shape((cols, 2, modes), f32),
    )((), table_re, table_im, mobility, *gathered)
    return surface, spectrum


def solution(mesh):
    in_specs = (
        P(("groups", "row"), "col"),
        P(("groups", "row"), "col"),
        P(("groups", "row"), "col"),
        P(None, ("groups", "row"), "col"),
    )
    out_specs = (P(("groups", "row"), "col"), P(("groups", "col"), None, "row"))
    return jax.shard_map(
        on_device, mesh=mesh, in_specs=in_specs, out_specs=out_specs, check_vma=False
    )
```

time: 141 us -> 93.8 us (0.67)
  Pallas kernels: 0 us -> 46 us
  waiting for transfers between devices: 48.9 us -> 14.6 us
  other arithmetic: 37.1 us -> 9.07 us
  between operations: 14.3 us -> 0.87 us
  local copies, waits for them, and re-layouts: 18.5 us -> 6.11 us
  matrix products: 7.34 us -> 0 us
  starting transfers between devices: 13.9 us -> 16.7 us
    pallas_call x0 -> x5, Pallas kernels: none -> 46 us  [run(): pl.pallas_call(body, out_shape=out_shape, in_specs=[pl.BlockSpec(memory_s...]
    reduce_scatter x1 -> x0, waiting for transfers between devices: 29.6 us -> none  [on_device(): lax.psum_scatter(wave_terms(jnp.int32(0), local_cols * lax.axis_size('col...]
    all_to_all x2 -> x0, waiting for transfers between devices: 17.2 us -> none  [the longest x1 9.58 us: on_device(): lax.all_to_all(velocity, 'row', split_axis=1, concat_axis=0, tiled=True)]
    ppermute x4 -> x15, waiting for transfers between devices: 2.11 us -> 14.6 us  [the longest x6 7.81 us: swap(): lax.ppermute(pieces[s], 'row', [(i, i ^ s) for i in range(row_count)])]
    ppermute x4 -> x15, starting transfers between devices: 6.92 us -> 16.7 us  [the longest x6 8.77 us: swap(): lax.ppermute(pieces[s], 'row', [(i, i ^ s) for i in range(row_count)])]
    add x6 -> x3, other arithmetic: 7.85 us -> 0.02 us  [the longest x2 0.01 us: on_device(): owner * cols + within]
    dot_general x6 -> x0, matrix products: 7.34 us -> none  [the longest x2 4.85 us: on_device(): lax.dot_general(columns, cosines, (((0,), (1,)), ((), ())), preferred_ele...]
    div x4 -> x0, other arithmetic: 7.01 us -> none  [substep(): curvature = lap_four(padded) / (metric * jnp.sqrt(metric))]
  transfers between devices with their start and end apart: 7 -> 15, of which waited for: 5 -> 7; matrix products, arithmetic and copies ran while one was open for 10% -> 9% of each run, Pallas kernels for 0% -> 2%
where the time goes in v1:
time: 93.8 us; the launch traced here: 93.4 us
  Pallas kernels  46 us (49%)
  starting transfers between devices  16.7 us (18%)
  waiting for transfers between devices  14.6 us (16%)
  other arithmetic  9.07 us (10%)
  local copies, waits for them, and re-layouts  6.11 us (7%)
    pallas_call x5, Pallas kernels, run(): pl.pallas_call(body, out_shape=out_shape, in_specs=[pl.BlockSpec(memory_s...  46 us
    ppermute x6, starting transfers between devices, swap(): lax.ppermute(pieces[s], 'row', [(i, i ^ s) for i in range(row_count)])  8.77 us
    ppermute x6, waiting for transfers between devices, swap(): lax.ppermute(pieces[s], 'row', [(i, i ^ s) for i in range(row_count)])  7.81 us
    unnamed x28, local copies, waits for them, and re-layouts  3.9 us
    ppermute x1, waiting for transfers between devices, on_device(): lax.ppermute(mine, 'col', [(i, (i - 2 * m) % col_count) for i in range(co...  3.88 us
    ppermute x1, starting transfers between devices, on_device(): above = lax.ppermute(down, 'row', ring_up)  3.05 us
    ppermute x1, waiting for transfers between devices, on_device(): outer_corner = lax.ppermute(outer_corner, 'col', across)  2.3 us
    slice x1, local copies, waits for them, and re-layouts, on_device(): forcing[:substeps - 1]  2.09 us
  transfers between devices with their start and end apart: 15, of which 7 were waited for; matrix products, arithmetic and copies ran while one was open for 9% of the time, Pallas kernels for 2%

profile of v1, /device:TPU:0, one launch (start us, length us, event | category | flops | bytes accessed | tf_op | source)
XLA Modules:
  0.0 93.4 jit_solution(6335431632402275445)
XLA Ops:
  0.6 2.1 %slice.3.f_ref = bf16[3,512,256]{2,1,0:T(8,128)(2,1)} slice(bf16[4,512,256]{2,1,0:T(8,128)(2,1)} %f_ref.1), slice={[0:3], [0:512], [0:256]} | slice | bytes 1572864 | tf_op jit(solution)/shard_map/slice | solution.py:345
  2.7 4.0 %shard_map.59 = (f32[64,256]{1,0:T(8,128)}, f32[64,256]{1,0:T(8,128)}, f32[256,128]{1,0:T(8,128)}, f32[256,128]{1,0:T(8,128)}) custom-call(s32[1]{0:T(128)} %bitcast.odd_ref, f32[512,256]{1,0:T(8,128)} %h_ref.3, f32[512,256]{1,0:T(8,128)} %g_ref.3, f32[512,256]{1,0:T(8,128)} %a_ref.3, bf16[3,512,256]{2,1,0:T(8,128)(2,1)} %slice.3.f_ref), custom_call_target="tpu_custom_call" | custom-call | tf_op jit(solution)/shard_map/pallas_call | solution.py:298
  6.8 3.1 %collective-permute-start = (f32[64,256]{1,0:T(8,128)}, f32[64,256]{1,0:T(8,128)S(1)}, u32[]{:S(2)}, u32[]{:S(2)}) collective-permute-start(f32[64,256]{1,0:T(8,128)} %get-tuple-element.17), channel_id=1, source_target_pairs={{0,4},{4,8},{8,12},{12,0},{1,5},{5,9},{9,13},{13,1},{2,6},{6,10},{... | collective-permute-start | bytes 196616 | tf_op jit(solution)/shard_map/ppermute | solution.py:346
  9.8 2.0 %collective-permute-start.1 = (f32[64,256]{1,0:T(8,128)}, f32[64,256]{1,0:T(8,128)S(1)}, u32[]{:S(2)}, u32[]{:S(2)}) collective-permute-start(f32[64,256]{1,0:T(8,128)} %get-tuple-element.18), channel_id=1, source_target_pairs={{0,12},{4,0},{8,4},{12,8},{1,13},{5,1},{9,5},{13,9},{2,14},{6,2},{... | collective-permute-start | bytes 196616 | tf_op jit(solution)/shard_map/ppermute | solution.py:347
  11.9 0.7 collective-permute-start.2
  12.5 1.2 %collective-permute-start.3 = (f32[256,128]{1,0:T(8,128)}, f32[256,128]{1,0:T(8,128)S(1)}, u32[]{:S(2)}, u32[]{:S(2)}) collective-permute-start(f32[256,128]{1,0:T(8,128)} %get-tuple-element.20), channel_id=1, source_target_pairs={{0,1},{1,0},{2,3},{3,2},{4,5},{5,4},{6,7},{7,6},{8,9},{9,8},{10,11... | collective-permute-start | bytes 393224 | tf_op jit(solution)/shard_map/ppermute | solution.py:349
  15.0 0.6 pad_maximum_fusion.1.phase_ref
  15.7 2.0 %add_convert_fusion = (bf16[16,32,1024]{2,1,0:T(8,128)(2,1)}, bf16[16,32,1024]{2,1,0:T(8,128)(2,1)}) fusion(f32[32,1024]{1,0:T(8,128)S(1)} %get-tuple-element.54, f32[16,1024]{1,0:T(8,128)S(1)} %get-tuple-element.43, f32[32,1024]{1,0:T(8,128)S(1)} %get-tuple-element.55, f32[16,1024]{1,0:T(8,128)S(1)} %get-tuple-element.42), kind=kLoop, calls=%fused_computation | loop fusion | flops 4194304 | bytes 2490368 | tf_op jit(solution)/shard_map/convert_element_type | solution.py:360
  18.3 0.6 copy-done.2
  18.9 1.6 %shard_map.60 = (f32[16,128]{1,0:T(8,128)}, f32[16,128]{1,0:T(8,128)}) custom-call(s32[1]{0:T(128)} %bitcast.odd_ref, f32[64,256]{1,0:T(8,128)} %copy-done.1, f32[64,256]{1,0:T(8,128)} %copy-done.2), custom_call_target="tpu_custom_call" | custom-call | tf_op jit(solution)/shard_map/pallas_call | solution.py:298
  21.5 2.3 %collective-permute-done.4.outer_corner_ref = f32[16,128]{1,0:T(8,128)S(1)} collective-permute-done((f32[16,128]{1,0:T(8,128)}, f32[16,128]{1,0:T(8,128)S(1)}, u32[]{:S(2)}, u32[]{:S(2)}) %collective-permute-start.4) | collective-permute-done | bytes 8224 | tf_op jit(solution)/shard_map/ppermute | solution.py:353
  24.4 0.7 copy-done.7
  25.1 33.8 %shard_map.61 = (f32[512,256]{1,0:T(8,128)}, bf16[64,512]{1,0:T(8,128)(2,1)}, bf16[64,512]{1,0:T(8,128)(2,1)}, bf16[64,512]{1,0:T(8,128)(2,1)}, bf16[64,512]{1,0:T(8,128)(2,1)}) custom-call(s32[2]{0:T(128)} %pad_add_fusion.1.place_ref, f32[512,256]{1,0:T(8,128)} %h_ref.3, f32[512,256]{1,0:T(8,128)} %g_ref.3, f32[512,256]{1,0:T(8,128)} %a_ref.3, ...), custom_call_target="tpu_custom_call" | custom-call | tf_op jit(solution)/shard_map/pallas_call | solution.py:298
  58.9 2.4 %collective-permute-start.7 = (bf16[64,512]{1,0:T(8,128)(2,1)}, bf16[64,512]{1,0:T(8,128)(2,1)S(1)}, u32[]{:S(2)}, u32[]{:S(2)}) collective-permute-start(bf16[64,512]{1,0:T(8,128)(2,1)} %get-tuple-element.26), channel_id=1, source_target_pairs={{0,8},{4,12},{8,0},{12,4},{1,9},{5,13},{9,1},{13,5},{2,10},{6,14},... | collective-permute-start | bytes 196616 | tf_op jit(solution)/shard_map/ppermute | solution.py:405
  61.3 2.0 %collective-permute-start.8 = (bf16[64,512]{1,0:T(8,128)(2,1)}, bf16[64,512]{1,0:T(8,128)(2,1)S(1)}, u32[]{:S(2)}, u32[]{:S(2)}) collective-permute-start(bf16[64,512]{1,0:T(8,128)(2,1)} %get-tuple-element.27), channel_id=1, source_target_pairs={{0,12},{4,8},{8,4},{12,0},{1,13},{5,9},{9,5},{13,1},{2,14},{6,10},... | collective-permute-start | bytes 196616 | tf_op jit(solution)/shard_map/ppermute | solution.py:405
  63.3 1.0 %collective-permute-done.6.rest_1_ = bf16[64,512]{1,0:T(8,128)(2,1)S(1)} collective-permute-done((bf16[64,512]{1,0:T(8,128)(2,1)}, bf16[64,512]{1,0:T(8,128)(2,1)S(1)}, u32[]{:S(2)}, u32[]{:S(2)}) %collective-permute-start.6) | collective-permute-done | bytes 65568 | tf_op jit(solution)/shard_map/ppermute | solution.py:405
  64.3 3.5 %collective-permute-done.7.rest_2_ = bf16[64,512]{1,0:T(8,128)(2,1)S(1)} collective-permute-done((bf16[64,512]{1,0:T(8,128)(2,1)}, bf16[64,512]{1,0:T(8,128)(2,1)S(1)}, u32[]{:S(2)}, u32[]{:S(2)}) %collective-permute-start.7) | collective-permute-done | bytes 65568 | tf_op jit(solution)/shard_map/ppermute | solution.py:405
  67.8 0.6 copy-done.9
  68.4 3.1 %shard_map.62 = (bf16[2,64,256]{2,1,0:T(8,128)(2,1)}, bf16[2,64,256]{2,1,0:T(8,128)(2,1)}, bf16[2,64,256]{2,1,0:T(8,128)(2,1)}, bf16[2,64,256]{2,1,0:T(8,128)(2,1)}) custom-call(s32[1]{0:T(128)} %bitcast.1.own_ref, f32[8,1024]{1,0:T(8,128)} %pad_maximum_fusion.1.phase_ref, bf16[512,1024]{1,0:T(8,128)(2,1)} %bitcast.14, bf16[512,1024]{1,0:T(8,128)(2,1)} %bitcast.13, ...), custom_call_target="tpu_custom_call" | custom-call | tf_op jit(solution)/shard_map/pallas_call | solution.py:298
  71.5 1.2 %collective-permute-start.9 = (bf16[2,64,256]{2,1,0:T(8,128)(2,1)}, bf16[2,64,256]{2,1,0:T(8,128)(2,1)S(1)}, u32[]{:S(2)}, u32[]{:S(2)}) collective-permute-start(bf16[2,64,256]{2,1,0:T(8,128)(2,1)} %get-tuple-element.29), channel_id=1, source_target_pairs={{0,4},{4,0},{8,12},{12,8},{1,5},{5,1},{9,13},{13,9},{2,6},{6,2},{1... | collective-permute-start | bytes 196616 | tf_op jit(solution)/shard_map/ppermute | solution.py:405
  72.7 1.2 %collective-permute-start.10 = (bf16[2,64,256]{2,1,0:T(8,128)(2,1)}, bf16[2,64,256]{2,1,0:T(8,128)(2,1)S(1)}, u32[]{:S(2)}, u32[]{:S(2)}) collective-permute-start(bf16[2,64,256]{2,1,0:T(8,128)(2,1)} %get-tuple-element.30), channel_id=1, source_target_pairs={{0,8},{4,12},{8,0},{12,4},{1,9},{5,13},{9,1},{13,5},{2,10},{6,14},... | collective-permute-start | bytes 196616 | tf_op jit(solution)/shard_map/ppermute | solution.py:405
  74.0 1.9 %collective-permute-start.11 = (bf16[2,64,256]{2,1,0:T(8,128)(2,1)}, bf16[2,64,256]{2,1,0:T(8,128)(2,1)S(1)}, u32[]{:S(2)}, u32[]{:S(2)}) collective-permute-start(bf16[2,64,256]{2,1,0:T(8,128)(2,1)} %get-tuple-element.31), channel_id=1, source_target_pairs={{0,12},{4,8},{8,4},{12,0},{1,13},{5,9},{9,5},{13,1},{2,14},{6,10},... | collective-permute-start | bytes 196616 | tf_op jit(solution)/shard_map/ppermute | solution.py:405
  75.9 1.1 %fusion.16 = (f32[16,2048]{1,0:T(8,128)S(1)}, f32[16,2048]{1,0:T(8,128)S(1)}, f32[16,2048]{1,0:T(8,128)S(1)}, f32[16,2048]{1,0:T(8,128)S(1)}) fusion(s32[2048]{0:T(1024)S(1)} %bitcast.21, s32[2048]{0:T(1024)S(1)} %pad_add_fusion, s32[16]{0:T(128)S(1)} %multiply_add_fusion), kind=kLoop, calls=%fused_computation.34 | loop fusion | flops 983040 | bytes 540736 | tf_op jit(solution)/shard_map/cos | solution.py:284
  77.0 2.1 %collective-permute-done.10 = bf16[2,64,256]{2,1,0:T(8,128)(2,1)S(1)} collective-permute-done((bf16[2,64,256]{2,1,0:T(8,128)(2,1)}, bf16[2,64,256]{2,1,0:T(8,128)(2,1)S(1)}, u32[]{:S(2)}, u32[]{:S(2)}) %collective-permute-start.10) | collective-permute-done | bytes 65568 | tf_op jit(solution)/shard_map/ppermute | solution.py:405
  79.1 1.2 %collective-permute-done.11 = bf16[2,64,256]{2,1,0:T(8,128)(2,1)S(1)} collective-permute-done((bf16[2,64,256]{2,1,0:T(8,128)(2,1)}, bf16[2,64,256]{2,1,0:T(8,128)(2,1)S(1)}, u32[]{:S(2)}, u32[]{:S(2)}) %collective-permute-start.11) | collective-permute-done | bytes 65568 | tf_op jit(solution)/shard_map/ppermute | solution.py:405
  80.3 0.9 pad_maximum_fusion.rest_0_
  81.8 2.0 %negate_convert_fusion = (bf16[16,16,2048]{2,1,0:T(8,128)(2,1)}, bf16[16,16,2048]{2,1,0:T(8,128)(2,1)}) fusion(f32[16,2048]{1,0:T(8,128)S(1)} %get-tuple-element.40, f32[16,2048]{1,0:T(8,128)S(1)} %get-tuple-element.39, f32[16,2048]{1,0:T(8,128)S(1)} %get-tuple-element.41, f32[16,2048]{1,0:T(8,128)S(1)} %get-tuple-element.38), kind=kLoop, calls=%fused_computation.2 | loop fusion | flops 4718592 | bytes 2621440 | tf_op jit(solution)/shard_map/convert_element_type | solution.py:380
  83.8 3.9 %collective-permute-done.12.rest_1_ = bf16[512,256]{1,0:T(8,128)(2,1)S(1)} collective-permute-done((bf16[512,256]{1,0:T(8,128)(2,1)S(1)}, bf16[512,256]{1,0:T(8,128)(2,1)S(1)}, u32[]{:S(2)}, u32[]{:S(2)}) %collective-permute-start.12) | collective-permute-done | bytes 262176 | tf_op jit(solution)/shard_map/ppermute | solution.py:419
  87.7 0.9 divide_multiply_fusion.mobility_ref
  88.5 0.6 collective-permute-done.14.rest_3_
  89.3 0.6 copy-done.5
  89.9 3.5 %shard_map.63 = f32[256,2,256]{2,1,0:T(2,128)} custom-call(bf16[256,2048]{1,0:T(8,128)(2,1)} %bitcast.16, bf16[256,2048]{1,0:T(8,128)(2,1)} %bitcast.15, f32[256,256]{1,0:T(8,128)} %divide_multiply_fusion.mobility_ref, bf16[512,256]{1,0:T(8,128)(2,1)} %copy-done, bf16[512,256]{1,0:T(8,128)(2,1)} %copy-done.3, bf16[512,256]{1,0:T(8,128)(2,1)} %copy-done.4, ...), custom_call_target="tpu_custom_call" | custom-call | tf_op jit(solution)/shard_map/pallas_call | solution.py:298
  (52 shorter events, 4.1 us)
Async XLA Ops:
  6.8 10.9 %collective-permute-start = (f32[64,256]{1,0:T(8,128)}, f32[64,256]{1,0:T(8,128)S(1)}, u32[]{:S(2)}, u32[]{:S(2)}) collective-permute-start(f32[64,256]{1,0:T(8,128)} %get-tuple-element.17), channel_id=1, source_target_pairs={{0,4},{4,8},{8,12},{12,0},{1,5},{5,9},{9,13},{13,1},{2,6},{6,10},{... | collective-permute-start | bytes 196616 | tf_op jit(solution)/shard_map/ppermute | solution.py:346
  9.8 7.8 %collective-permute-start.1 = (f32[64,256]{1,0:T(8,128)}, f32[64,256]{1,0:T(8,128)S(1)}, u32[]{:S(2)}, u32[]{:S(2)}) collective-permute-start(f32[64,256]{1,0:T(8,128)} %get-tuple-element.18), channel_id=1, source_target_pairs={{0,12},{4,0},{8,4},{12,8},{1,13},{5,1},{9,5},{13,9},{2,14},{6,2},{... | collective-permute-start | bytes 196616 | tf_op jit(solution)/shard_map/ppermute | solution.py:347
  11.9 11.9 %collective-permute-start.2 = (f32[256,128]{1,0:T(8,128)}, f32[256,128]{1,0:T(8,128)S(1)}, u32[]{:S(2)}, u32[]{:S(2)}) collective-permute-start(f32[256,128]{1,0:T(8,128)} %get-tuple-element.19), channel_id=1, source_target_pairs={{0,3},{1,2},{2,1},{3,0},{4,7},{5,6},{6,5},{7,4},{8,11},{9,10},{10,... | collective-permute-start | bytes 393224 | tf_op jit(solution)/shard_map/ppermute | solution.py:348
  12.5 11.3 %collective-permute-start.3 = (f32[256,128]{1,0:T(8,128)}, f32[256,128]{1,0:T(8,128)S(1)}, u32[]{:S(2)}, u32[]{:S(2)}) collective-permute-start(f32[256,128]{1,0:T(8,128)} %get-tuple-element.20), channel_id=1, source_target_pairs={{0,1},{1,0},{2,3},{3,2},{4,5},{5,4},{6,7},{7,6},{8,9},{9,8},{10,11... | collective-permute-start | bytes 393224 | tf_op jit(solution)/shard_map/ppermute | solution.py:349
  17.6 0.6 copy-start.1
  18.3 0.6 copy-start.2
  20.5 3.3 %collective-permute-start.4 = (f32[16,128]{1,0:T(8,128)}, f32[16,128]{1,0:T(8,128)S(1)}, u32[]{:S(2)}, u32[]{:S(2)}) collective-permute-start(f32[16,128]{1,0:T(8,128)} %get-tuple-element.21), channel_id=1, source_target_pairs={{0,3},{1,2},{2,1},{3,0},{4,7},{5,6},{6,5},{7,4},{8,11},{9,10},{10,... | collective-permute-start | bytes 24584 | tf_op jit(solution)/shard_map/ppermute | solution.py:353
  20.5 3.3 %collective-permute-start.5 = (f32[16,128]{1,0:T(8,128)}, f32[16,128]{1,0:T(8,128)S(1)}, u32[]{:S(2)}, u32[]{:S(2)}) collective-permute-start(f32[16,128]{1,0:T(8,128)} %get-tuple-element.22), channel_id=1, source_target_pairs={{0,1},{1,0},{2,3},{3,2},{4,5},{5,4},{6,7},{7,6},{8,9},{9,8},{10,11... | collective-permute-start | bytes 24584 | tf_op jit(solution)/shard_map/ppermute | solution.py:354
  23.8 0.6 copy-start.11
  23.8 0.6 copy-start.12
  23.8 0.7 copy-start.6
  24.4 0.7 copy-start.7
  58.9 5.4 %collective-permute-start.6 = (bf16[64,512]{1,0:T(8,128)(2,1)}, bf16[64,512]{1,0:T(8,128)(2,1)S(1)}, u32[]{:S(2)}, u32[]{:S(2)}) collective-permute-start(bf16[64,512]{1,0:T(8,128)(2,1)} %get-tuple-element.25), channel_id=1, source_target_pairs={{0,4},{4,0},{8,12},{12,8},{1,5},{5,1},{9,13},{13,9},{2,6},{6,2},{1... | collective-permute-start | bytes 196616 | tf_op jit(solution)/shard_map/ppermute | solution.py:405
  58.9 8.8 %collective-permute-start.7 = (bf16[64,512]{1,0:T(8,128)(2,1)}, bf16[64,512]{1,0:T(8,128)(2,1)S(1)}, u32[]{:S(2)}, u32[]{:S(2)}) collective-permute-start(bf16[64,512]{1,0:T(8,128)(2,1)} %get-tuple-element.26), channel_id=1, source_target_pairs={{0,8},{4,12},{8,0},{12,4},{1,9},{5,13},{9,1},{13,5},{2,10},{6,14},... | collective-permute-start | bytes 196616 | tf_op jit(solution)/shard_map/ppermute | solution.py:405
  61.3 6.5 %collective-permute-start.8 = (bf16[64,512]{1,0:T(8,128)(2,1)}, bf16[64,512]{1,0:T(8,128)(2,1)S(1)}, u32[]{:S(2)}, u32[]{:S(2)}) collective-permute-start(bf16[64,512]{1,0:T(8,128)(2,1)} %get-tuple-element.27), channel_id=1, source_target_pairs={{0,12},{4,8},{8,4},{12,0},{1,13},{5,9},{9,5},{13,1},{2,14},{6,10},... | collective-permute-start | bytes 196616 | tf_op jit(solution)/shard_map/ppermute | solution.py:405
  64.3 3.5 %copy-start.8 = (bf16[64,512]{1,0:T(8,128)(2,1)}, bf16[64,512]{1,0:T(8,128)(2,1)S(1)}, u32[]{:S(2)}) copy-start(bf16[64,512]{1,0:T(8,128)(2,1)S(1)} %collective-permute-done.6.rest_1_) | copy-start | bytes 196612
  67.8 0.6 copy-start.9
  67.8 0.6 copy-start.10
  71.5 5.5 %collective-permute-start.9 = (bf16[2,64,256]{2,1,0:T(8,128)(2,1)}, bf16[2,64,256]{2,1,0:T(8,128)(2,1)S(1)}, u32[]{:S(2)}, u32[]{:S(2)}) collective-permute-start(bf16[2,64,256]{2,1,0:T(8,128)(2,1)} %get-tuple-element.29), channel_id=1, source_target_pairs={{0,4},{4,0},{8,12},{12,8},{1,5},{5,1},{9,13},{13,9},{2,6},{6,2},{1... | collective-permute-start | bytes 196616 | tf_op jit(solution)/shard_map/ppermute | solution.py:405
  72.7 6.4 %collective-permute-start.10 = (bf16[2,64,256]{2,1,0:T(8,128)(2,1)}, bf16[2,64,256]{2,1,0:T(8,128)(2,1)S(1)}, u32[]{:S(2)}, u32[]{:S(2)}) collective-permute-start(bf16[2,64,256]{2,1,0:T(8,128)(2,1)} %get-tuple-element.30), channel_id=1, source_target_pairs={{0,8},{4,12},{8,0},{12,4},{1,9},{5,13},{9,1},{13,5},{2,10},{6,14},... | collective-permute-start | bytes 196616 | tf_op jit(solution)/shard_map/ppermute | solution.py:405
  74.0 6.4 %collective-permute-start.11 = (bf16[2,64,256]{2,1,0:T(8,128)(2,1)}, bf16[2,64,256]{2,1,0:T(8,128)(2,1)S(1)}, u32[]{:S(2)}, u32[]{:S(2)}) collective-permute-start(bf16[2,64,256]{2,1,0:T(8,128)(2,1)} %get-tuple-element.31), channel_id=1, source_target_pairs={{0,12},{4,8},{8,4},{12,0},{1,13},{5,9},{9,5},{13,1},{2,14},{6,10},... | collective-permute-start | bytes 196616 | tf_op jit(solution)/shard_map/ppermute | solution.py:405
  81.2 2.6 %copy-start = (bf16[512,256]{1,0:T(8,128)(2,1)}, bf16[512,256]{1,0:T(8,128)(2,1)S(1)}, u32[]{:S(2)}) copy-start(bf16[512,256]{1,0:T(8,128)(2,1)S(1)} %pad_maximum_fusion.rest_0_) | copy-start | bytes 786436
  81.2 6.4 %collective-permute-start.12 = (bf16[512,256]{1,0:T(8,128)(2,1)S(1)}, bf16[512,256]{1,0:T(8,128)(2,1)S(1)}, u32[]{:S(2)}, u32[]{:S(2)}) collective-permute-start(bf16[512,256]{1,0:T(8,128)(2,1)S(1)} %pad_maximum_fusion.rest_0_), channel_id=1, source_target_pairs={{0,2},{1,3},{2,0},{3,1},{4,6},{5,7},{6,4},{7,5},{8,10},{9,11},{10,... | collective-permute-start | bytes 786440 | tf_op jit(solution)/shard_map/ppermute | solution.py:419
  83.8 4.8 %collective-permute-start.13 = (bf16[512,256]{1,0:T(8,128)(2,1)S(1)}, bf16[512,256]{1,0:T(8,128)(2,1)S(1)}, u32[]{:S(2)}, u32[]{:S(2)}) collective-permute-start(bf16[512,256]{1,0:T(8,128)(2,1)S(1)} %pad_maximum_fusion.rest_0_), channel_id=1, source_target_pairs={{0,1},{1,0},{2,3},{3,2},{4,5},{5,4},{6,7},{7,6},{8,9},{9,8},{10,11... | collective-permute-start | bytes 786440 | tf_op jit(solution)/shard_map/ppermute | solution.py:422
  87.6 1.5 %copy-start.3 = (bf16[512,256]{1,0:T(8,128)(2,1)}, bf16[512,256]{1,0:T(8,128)(2,1)S(1)}, u32[]{:S(2)}) copy-start(bf16[512,256]{1,0:T(8,128)(2,1)S(1)} %collective-permute-done.12.rest_1_) | copy-start | bytes 786436
  87.6 1.5 %collective-permute-start.14 = (bf16[512,256]{1,0:T(8,128)(2,1)S(1)}, bf16[512,256]{1,0:T(8,128)(2,1)S(1)}, u32[]{:S(2)}, u32[]{:S(2)}) collective-permute-start(bf16[512,256]{1,0:T(8,128)(2,1)S(1)} %collective-permute-done.12.rest_1_), channel_id=1, source_target_pairs={{0,1},{1,0},{2,3},{3,2},{4,5},{5,4},{6,7},{7,6},{8,9},{9,8},{10,11... | collective-permute-start | bytes 786440 | tf_op jit(solution)/shard_map/ppermute | solution.py:422
  88.5 0.7 copy-start.4
  89.2 0.7 copy-start.5

commit v2 on v1

--- a/solution.py
+++ b/solution.py
@@ -36,7 +36,7 @@
 def pack_kernel(plan, odd_ref, h_ref, g_ref, a_ref, f_ref, up_ref, down_ref, outer_ref, inner_ref):
     rows, cols = h_ref.shape
     odd = odd_ref[0] == 1
-    sources = [h_ref, g_ref, a_ref] + [f_ref.at[s] for s in range(f_ref.shape[0])]
+    sources = [h_ref, g_ref, a_ref] + [f_ref.at[s] for s in range(len(plan) - 3)]
     for (width, offset), ref in zip(plan, sources):
         up_ref[offset : offset + width, :] = ref[0:16, :].astype(jnp.float32)[:width]
         down_ref[offset : offset + width, :] = ref[rows - 16 : rows, :].astype(jnp.float32)[16 - width :]
@@ -61,7 +61,7 @@
         inner_ref[pl.ds(place, 16), :] = jnp.where(odd, left, right)
         return carry
 
-    lax.fori_loop(0, half // 16, body, 0)
+    lax.fori_loop(0, half // 16, body, 0, unroll=2)
 
 
 def corner_kernel(odd_ref, above_ref, below_ref, outer_ref, inner_ref):
@@ -81,158 +81,293 @@
     inner_ref[...] = jnp.where(odd, left, right)
 
 
-def evolve_kernel(
+def gains_of(substeps):
+    return [1.0, step_size * 12.0, step_size] + [step_size] * substeps
+
+
+def scaled(value, gain):
+    return value if gain == 1.0 else value * gain
+
+
+SHIFTS = (1, 2, -1, -2)
+
+
+def segment(rows):
+    return -(-rows // SUBLANES) | 1
+
+
+def unrolling(seg, most):
+    return max(u for u in range(1, most + 1) if seg % u == 0)
+
+
+def evolve(surf_ref, curv_ref, coefficient, store, tiles, kept, seg, substeps, unroll):
+    lane = lane_ids()
+    masks = {shift: (lane < shift if shift > 0 else lane >= LANES + shift) for shift in SHIFTS}
+
+    def wrap_rows(ref):
+        for tile in range(tiles):
+            for t in range(2):
+                ref[tile, t] = pltpu.roll(ref[tile, seg + t], 1, 0)
+                ref[tile, seg + 2 + t] = pltpu.roll(ref[tile, 2 + t], SUBLANES - 1, 0)
+
+    def turned(ref, t):
+        return tuple(rolled(ref[tile, t + 2], shift) for shift in SHIFTS for tile in range(tiles))
+
+    def shifted(turns, tile):
+        result = []
+        for n, shift in enumerate(SHIFTS):
+            mine = turns[n * tiles + tile]
+            if tiles > 1:
+                mine = jnp.where(masks[shift], turns[n * tiles + (tile + (-1 if shift > 0 else 1)) % tiles], mine)
+            result.append(mine)
+        return result
+
+    def sweep(ref, emit):
+        def body(i, turns):
+            for u in range(unroll):
+                t = i * unroll + u
+                ahead = turned(ref, t + 1)
+                emit(t, turns)
+                turns = ahead
+            return turns
+
+        lax.fori_loop(0, seg // unroll, body, turned(ref, 0))
+
+    def stencil(ref, tile, t, turns):
+        back_one, back_two, next_one, next_two = shifted(turns, tile)
+        up_two, up_one, mid = ref[tile, t], ref[tile, t + 1], ref[tile, t + 2]
+        down_one, down_two = ref[tile, t + 3], ref[tile, t + 4]
+        near = (back_one + next_one) + (up_one + down_one)
+        far = (back_two + next_two) + (up_two + down_two)
+        lap = 16.0 * near - far - 60.0 * mid
+        return lap, (back_one, back_two, next_one, next_two, up_two, up_one, down_one, down_two)
+
+    def bend(t, turns):
+        for tile in range(tiles):
+            lap, (back_one, back_two, next_one, next_two, up_two, up_one, down_one, down_two) = stencil(
+                surf_ref, tile, t, turns
+            )
+            slope_c = 8.0 * (next_one - back_one) - (next_two - back_two)
+            slope_r = 8.0 * (down_one - up_one) - (down_two - up_two)
+            root = lax.rsqrt(slope_c * slope_c + slope_r * slope_r + 144.0)
+            curv_ref[tile, t + 2] = lap * (root * root * root)
+
+    def update(s, t, turns):
+        for tile in range(kept if s == substeps - 1 else tiles):
+            lap, _ = stencil(curv_ref, tile, t, turns)
+            center = surf_ref[tile, t + 2]
+            binding = (coefficient(2, tile, t) * center) * jnp.exp(-0.5 * center * center)
+            value = center + (coefficient(3 + s, tile, t) - coefficient(1, tile, t) * lap - binding)
+            if s == substeps - 1:
+                store(tile, t, value)
+            else:
+                surf_ref[tile, t + 2] = value
+
+    for s in range(substeps):
+        wrap_rows(surf_ref)
+        sweep(surf_ref, bend)
+        wrap_rows(curv_ref)
+        sweep(curv_ref, functools.partial(update, s))
+
+
+def inner_kernel(substeps, h_ref, g_ref, a_ref, f_ref, flat_ref, side_ref, band_ref, part_ref, surf_ref, curv_ref):
+    rows, cols = h_ref.shape
+    tiles = cols // LANES
+    seg = segment(rows)
+    reach = 4 * substeps
+    lane = lane_ids()
+    gains = gains_of(substeps)
+    sources = [h_ref, g_ref, a_ref] + [f_ref.at[s] for s in range(substeps)]
+    for n, ref in enumerate(sources):
+        for tile in range(tiles):
+            block = ref[:, tile * LANES : (tile + 1) * LANES].astype(jnp.float32)
+            part_ref[n, tile, 0:rows, :] = scaled(block, gains[n])
+            part_ref[n, tile, rows:, :] = jnp.zeros((SUBLANES * seg - rows, LANES), jnp.float32)
+    for n in range(len(sources)):
+        for tile in range(tiles):
+            band_ref[n, tile, 0 : 2 * reach, :] = part_ref[n, tile, 0 : 2 * reach, :]
+            band_ref[n, tile, 2 * reach : 4 * reach, :] = part_ref[n, tile, rows - 2 * reach : rows, :]
+
+        def edge(i, carry):
+            place = pl.ds(pl.multiple_of(i * 16, 16), 16)
+            first = rolled(part_ref[n, 0, place, :], 3 * reach)
+            side_ref[n, place, :] = jnp.where(lane < 6 * reach, first, part_ref[n, tiles - 1, place, :])
+            return carry
+
+        lax.fori_loop(0, rows // 16, edge, 0, unroll=4)
+
+    def spread(t, carry):
+        for tile in range(tiles):
+            surf_ref[tile, t + 2] = part_ref[0, tile, pl.ds(t, SUBLANES, stride=seg), :]
+        return carry
+
+    lax.fori_loop(0, seg, spread, 0, unroll=unrolling(seg, 5))
+
+    def coefficient(n, tile, t):
+        return part_ref[n, tile, pl.ds(t, SUBLANES, stride=seg), :]
+
+    def store(tile, t, value):
+        flat_ref[tile, pl.ds(t, SUBLANES, stride=seg), :] = value
+
+    evolve(surf_ref, curv_ref, coefficient, store, tiles, tiles, seg, substeps, unrolling(seg, 13))
+
+
+def edge_kernel(
     plan,
     substeps,
-    place_ref,
-    h_ref,
-    g_ref,
-    a_ref,
-    f_ref,
+    odd_ref,
+    side_own_ref,
+    band_own_ref,
     above_ref,
     below_ref,
     outer_ref,
     inner_ref,
-    outer_corner_ref,
-    inner_corner_ref,
-    *rest,
+    side_ref,
+    band_ref,
 ):
-    slots = len(rest) - 5
-    new_ref = rest[0]
-    slot_refs = rest[1 : slots]
-    ext_ref, surf_ref, curv_ref, flat_ref, turned_ref = rest[slots:]
-    rows, cols = h_ref.shape
-    tiles = cols // LANES
-    odd = place_ref[0] == 1
-    own = place_ref[1]
+    rows = side_own_ref.shape[1]
+    tiles = band_own_ref.shape[1]
     depth = 4 * substeps
-    total = rows + 2 * depth
-    seg = total // SUBLANES
+    half = rows // 2
+    odd = odd_ref[0] == 1
     lane = lane_ids()
-    gains = [1.0, step_size * 12.0, step_size] + [step_size] * substeps
-    sources = [h_ref, g_ref, a_ref] + [f_ref.at[s] for s in range(substeps)]
-
-    for n, ref in enumerate(sources):
-        for tile in range(tiles):
-            block = ref[:, tile * LANES : (tile + 1) * LANES].astype(jnp.float32)
-            ext_ref[n, tile, depth : depth + rows, :] = block if gains[n] == 1.0 else block * gains[n]
-    half = rows // 2
+    gains = gains_of(substeps)
 
     def side(i, carry):
-        start = pl.multiple_of(i * 16, 16)
-        outer = outer_ref[pl.ds(start, 16), :]
-        inner = inner_ref[pl.ds(start, 16), :]
+        start = pl.ds(pl.multiple_of(i * 16, 16), 16)
+        outer, inner = outer_ref[start, :], inner_ref[start, :]
         on_right = jnp.where(odd, outer, inner)
         on_left = jnp.where(odd, inner, outer)
         for n, (width, offset) in enumerate(plan):
             for part in range(2):
                 at = offset + part * (LANES // 2)
-                value = jnp.where(lane < width, rolled(on_right, -at), 0.0)
-                value = jnp.where(lane >= LANES - width, rolled(on_left, -at - width), value)
-                place = pl.multiple_of(depth + part * half + i * 16, 8)
-                ext_ref[n, tiles, pl.ds(place, 16), :] = value if gains[n] == 1.0 else value * gains[n]
+                place = pl.multiple_of(part * half + i * 16, 8)
+                value = scaled(rolled(on_right, -at), gains[n])
+                left = scaled(rolled(on_left, 3 * depth - width - at), gains[n])
+                value = jnp.where((lane >= 3 * depth - width) & (lane < 3 * depth), left, value)
+                keep = (lane < width) | ((lane >= 3 * depth - width) & (lane < 3 * depth))
+                value = jnp.where(keep, value, side_own_ref[n, pl.ds(place, 16), :])
+                side_ref[n, pl.ds(place + depth, 16), :] = value
         return carry
 
-    lax.fori_loop(0, half // 16, side, 0)
-    ext_ref[2 + substeps, tiles] = jnp.zeros((total, LANES), jnp.float32)
-
-    corner_right = jnp.where(odd, outer_corner_ref[...], inner_corner_ref[...])
-    corner_left = jnp.where(odd, inner_corner_ref[...], outer_corner_ref[...])
-    corner = []
-    for group in range(8):
-        value = jnp.where(lane < 16, rolled(corner_right, -16 * group), 0.0)
-        corner.append(jnp.where(lane >= LANES - 16, rolled(corner_left, -16 * group - 16), value))
-    above_tail = jnp.concatenate(corner[:4], axis=0)
-    below_tail = jnp.concatenate(corner[4:], axis=0)
-    for tile in range(tiles + 1):
-        if tile < tiles:
-            above = above_ref[:, tile * LANES : (tile + 1) * LANES]
-            below = below_ref[:, tile * LANES : (tile + 1) * LANES]
-        else:
-            above, below = above_tail, below_tail
+    lax.fori_loop(0, half // 16, side, 0, unroll=2)
+    last = len(plan)
+    side_ref[last] = jnp.zeros(side_ref.shape[1:], jnp.float32)
+    side_ref[last, depth : depth + rows, :] = side_own_ref[last]
+    for n in range(last + 1):
+        side_ref[n, rows + 2 * depth :, :] = jnp.zeros((side_ref.shape[1] - rows - 2 * depth, LANES), jnp.float32)
+        for tile in range(tiles + 1):
+            band_ref[n, tile, 0:depth, :] = jnp.zeros((depth, LANES), jnp.float32)
+            band_ref[n, tile, 5 * depth :, :] = jnp.zeros((band_ref.shape[2] - 5 * depth, LANES), jnp.float32)
+    for n in range(last + 1):
+        for tile in range(tiles):
+            band_ref[n, tile, depth : 5 * depth, :] = band_own_ref[n, tile]
+        for at, place in ((depth, depth), (depth + rows - 2 * depth, 3 * depth)):
+            value = side_ref[n, at : at + 2 * depth, :]
+            left = rolled(value, -3 * depth)
+            band_ref[n, tiles, place : place + 2 * depth, :] = jnp.where(lane < 4 * depth, value, left)
+    for tile in range(tiles):
+        span = slice(tile * LANES, (tile + 1) * LANES)
         for n, (width, offset) in enumerate(plan):
-            top = above[offset : offset + width]
-            bottom = below[offset : offset + width]
-            if gains[n] != 1.0:
-                top, bottom = top * gains[n], bottom * gains[n]
-            if width < depth:
-                pad = jnp.zeros((depth - width, LANES), jnp.float32)
-                top = jnp.concatenate([pad, top], axis=0)
-                bottom = jnp.concatenate([bottom, pad], axis=0)
-            ext_ref[n, tile, 0:depth, :] = top
-            ext_ref[n, tile, depth + rows : total, :] = bottom
-        pad = jnp.zeros((depth, LANES), jnp.float32)
-        ext_ref[2 + substeps, tile, 0:depth, :] = pad
-        ext_ref[2 + substeps, tile, depth + rows : total, :] = pad
-
-    def spread(t, carry):
+            band_ref[n, tile, depth - width : depth, :] = scaled(above_ref[offset : offset + width, span], gains[n])
+            band_ref[n, tile, 5 * depth : 5 * depth + width, :] = scaled(
+                below_ref[offset : offset + width, span], gains[n]
+            )
+    for n in range(last):
+        for at, place in ((0, 0), (5 * depth, depth + rows)):
+            first = rolled(band_ref[n, 0, at : at + depth, :], 3 * depth)
+            side_ref[n, place : place + depth, :] = jnp.where(
+                lane < 6 * depth, first, band_ref[n, tiles - 1, at : at + depth, :]
+            )
+
+
+def outer_kernel(
+    plan,
+    substeps,
+    place_ref,
+    side_in_ref,
+    band_in_ref,
+    outer_ref,
+    inner_ref,
+    flat_ref,
+    h_ref,
+    *rest,
+):
+    slots = len(rest) - 10
+    new_ref, slot_refs = rest[0], rest[1 : 1 + slots]
+    side_ref, band_ref, side_surf, side_curv, band_surf, band_curv, side_flat, band_flat, turned_ref = rest[-9:]
+    rows, cols = h_ref.shape
+    tiles = cols // LANES
+    depth = 4 * substeps
+    odd = place_ref[0] == 1
+    own = place_ref[1]
+    lane = lane_ids()
+    gains = gains_of(substeps)
+    side_seg = segment(rows + 2 * depth)
+    band_seg = segment(6 * depth)
+
+    side_ref[...] = side_in_ref[...]
+    band_ref[...] = band_in_ref[...]
+
+    corner_right = jnp.where(odd, outer_ref[...], inner_ref[...])
+    corner_left = jnp.where(odd, inner_ref[...], outer_ref[...])
+    rights = [rolled(corner_right, -16 * group) for group in range(8)]
+    lefts = [rolled(corner_left, -16 * group - 16) for group in range(8)]
+    for end in range(2):
+        right = jnp.concatenate(rights[4 * end : 4 * end + 4], axis=0)
+        left = jnp.concatenate(lefts[4 * end : 4 * end + 4], axis=0)
+        for n, (width, offset) in enumerate(plan):
+            both = jnp.where(lane < 4 * depth, right[offset : offset + width], left[offset : offset + width])
+            both = scaled(both, gains[n])
+            at = depth - width if end == 0 else 5 * depth
+            band_ref[n, tiles, at : at + width, :] = both
+            at = depth - width if end == 0 else depth + rows
+            moved = rolled(both, 3 * depth)
+            value = jnp.where((lane >= 2 * depth) & (lane < 3 * depth), moved, side_ref[n, at : at + width, :])
+            side_ref[n, at : at + width, :] = jnp.where(lane < depth, both, value)
+
+    def spread_side(t, carry):
+        side_surf[0, t + 2] = side_ref[0, pl.ds(t, SUBLANES, stride=side_seg), :]
+        return carry
+
+    lax.fori_loop(0, side_seg, spread_side, 0, unroll=unrolling(side_seg, 4))
+
+    def spread_band(t, carry):
         for tile in range(tiles + 1):
-            surf_ref[tile, t + 2] = ext_ref[0, tile, pl.ds(t, SUBLANES, stride=seg), :]
+            band_surf[tile, t + 2] = band_ref[0, tile, pl.ds(t, SUBLANES, stride=band_seg), :]
         return carry
 
-    lax.fori_loop(0, seg, spread, 0, unroll=4)
-
-    def wrap_rows(ref):
-        for tile in range(tiles + 1):
-            for t in range(2):
-                ref[tile, t] = pltpu.roll(ref[tile, seg + t], 1, 0)
-                ref[tile, seg + 2 + t] = pltpu.roll(ref[tile, 2 + t], SUBLANES - 1, 0)
-
-    masks = {shift: (lane < shift if shift > 0 else lane >= LANES + shift) for shift in (1, 2, -1, -2)}
-
-    def moved(values, shift):
-        turned = [rolled(v, shift) for v in values]
-        count = len(values)
-        step = -1 if shift > 0 else 1
-        return [jnp.where(masks[shift], turned[(i + step) % count], turned[i]) for i in range(count)]
-
-    def bend(t, carry):
-        mid = [surf_ref[tile, t + 2] for tile in range(tiles + 1)]
-        back_one, back_two = moved(mid, 1), moved(mid, 2)
-        next_one, next_two = moved(mid, -1), moved(mid, -2)
-        for tile in range(tiles + 1):
-            up_two, up_one = surf_ref[tile, t], surf_ref[tile, t + 1]
-            down_one, down_two = surf_ref[tile, t + 3], surf_ref[tile, t + 4]
-            near = (back_one[tile] + next_one[tile]) + (up_one + down_one)
-            far = (back_two[tile] + next_two[tile]) + (up_two + down_two)
-            lap = 16.0 * near - far - 60.0 * mid[tile]
-            slope_c = 8.0 * (next_one[tile] - back_one[tile]) - (next_two[tile] - back_two[tile])
-            slope_r = 8.0 * (down_one - up_one) - (down_two - up_two)
-            root = lax.rsqrt(slope_c * slope_c + slope_r * slope_r + 144.0)
-            curv_ref[tile, t + 2] = lap * (root * root * root)
-        return carry
-
-    def update(s, t, carry):
-        mid = [curv_ref[tile, t + 2] for tile in range(tiles + 1)]
-        back_one, back_two = moved(mid, 1), moved(mid, 2)
-        next_one, next_two = moved(mid, -1), moved(mid, -2)
-        for tile in range(tiles if s == substeps - 1 else tiles + 1):
-            up_two, up_one = curv_ref[tile, t], curv_ref[tile, t + 1]
-            down_one, down_two = curv_ref[tile, t + 3], curv_ref[tile, t + 4]
-            near = (back_one[tile] + next_one[tile]) + (up_one + down_one)
-            far = (back_two[tile] + next_two[tile]) + (up_two + down_two)
-            lap = 16.0 * near - far - 60.0 * mid[tile]
-            place = pl.ds(t, SUBLANES, stride=seg)
-            center = surf_ref[tile, t + 2]
-            binding = (ext_ref[2, tile, place, :] * center) * jnp.exp(-0.5 * center * center)
-            value = center + (ext_ref[3 + s, tile, place, :] - ext_ref[1, tile, place, :] * lap - binding)
-            if s == substeps - 1:
-                flat_ref[tile, place, :] = value
-            else:
-                surf_ref[tile, t + 2] = value
-        return carry
-
-    for s in range(substeps):
-        wrap_rows(surf_ref)
-        lax.fori_loop(0, seg, bend, 0, unroll=2)
-        wrap_rows(curv_ref)
-        lax.fori_loop(0, seg, functools.partial(update, s), 0, unroll=2)
+    lax.fori_loop(0, band_seg, spread_band, 0)
+
+    def side_coefficient(n, tile, t):
+        return side_ref[n, pl.ds(t, SUBLANES, stride=side_seg), :]
+
+    def side_store(tile, t, value):
+        side_flat[pl.ds(t, SUBLANES, stride=side_seg), :] = value
+
+    def band_coefficient(n, tile, t):
+        return band_ref[n, tile, pl.ds(t, SUBLANES, stride=band_seg), :]
+
+    def band_store(tile, t, value):
+        band_flat[tile, pl.ds(t, SUBLANES, stride=band_seg), :] = value
+
+    evolve(side_surf, side_curv, side_coefficient, side_store, 1, 1, side_seg, substeps, unrolling(side_seg, 23))
+    evolve(band_surf, band_curv, band_coefficient, band_store, tiles + 1, tiles, band_seg, substeps, unrolling(band_seg, 13))
 
     for tile in range(tiles):
-        fresh = flat_ref[tile, depth : depth + rows, :]
-        new_ref[:, tile * LANES : (tile + 1) * LANES] = fresh
-        speed = (fresh - h_ref[:, tile * LANES : (tile + 1) * LANES]) * (1.0 / (substeps * step_size))
-        turned_ref[tile * LANES : (tile + 1) * LANES, :] = jnp.transpose(speed).astype(jnp.bfloat16)
+        span = slice(tile * LANES, (tile + 1) * LANES)
+        fresh = flat_ref[tile, 0:rows, :]
+        sides = side_flat[depth : depth + rows, :]
+        if tile == 0:
+            fresh = jnp.where(lane < depth, rolled(sides, -3 * depth), fresh)
+        if tile == tiles - 1:
+            fresh = jnp.where(lane >= LANES - depth, sides, fresh)
+        top = band_flat[tile, depth : 2 * depth, :]
+        bottom = band_flat[tile, 4 * depth : 5 * depth, :]
+        fresh = jnp.concatenate([top, fresh[depth : rows - depth], bottom], axis=0)
+        new_ref[:, span] = fresh
+        speed = (fresh - h_ref[:, span]) * (1.0 / (substeps * step_size))
+        turned_ref[span, :] = jnp.transpose(speed).astype(jnp.bfloat16)
     share = cols // len(slot_refs)
     for s, ref in enumerate(slot_refs):
         ref[...] = turned_ref[pl.ds(pl.multiple_of((own ^ s) * share, share), share), :]
@@ -293,18 +428,23 @@
     return cosines.reshape(-1, span), sines.reshape(-1, span)
 
 
-def kernel_call(body, out_shape, scratch=(), **options):
+def kernel_call(body, out_shape, scratch=(), resident=(), **options):
+    vmem = pl.BlockSpec(memory_space=pltpu.VMEM)
+    single = isinstance(out_shape, jax.ShapeDtypeStruct)
+    out_shape = [out_shape] if single else list(out_shape)
+
     def run(scalars, *operands):
-        return pl.pallas_call(
+        outs = pl.pallas_call(
             body,
             out_shape=out_shape,
             in_specs=[pl.BlockSpec(memory_space=pltpu.SMEM)] * len(scalars)
-            + [pl.BlockSpec(memory_space=pltpu.VMEM)] * len(operands),
-            out_specs=jax.tree.map(lambda _: pl.BlockSpec(memory_space=pltpu.VMEM), out_shape),
+            + [vmem if n in resident else pl.BlockSpec() for n in range(len(operands))],
+            out_specs=[vmem if n - len(out_shape) in resident else pl.BlockSpec() for n in range(len(out_shape))],
             scratch_shapes=list(scratch),
             compiler_params=pltpu.CompilerParams(vmem_limit_bytes=56 * 1024 * 1024),
             **options,
         )(*scalars, *operands)
+        return outs[0] if single else outs
 
     return run
 
@@ -325,7 +465,6 @@
     tiles = cols // LANES
     depth = 4 * substeps
     total = rows + 2 * depth
-    seg = total // SUBLANES
     f32, bf16 = jnp.float32, jnp.bfloat16
     shape = jax.ShapeDtypeStruct
 
@@ -342,7 +481,7 @@
             shape((rows // 2, LANES), f32),
             shape((rows // 2, LANES), f32),
         ),
-    )((odd[None],), height, rigidity, adhesion, forcing[: substeps - 1])
+    )((odd[None],), height, rigidity, adhesion, forcing)
     above = lax.ppermute(down, "row", ring_up)
     below = lax.ppermute(up, "row", ring_down)
     outer = lax.ppermute(outer, "col", across)
@@ -388,17 +527,45 @@
     mobility = 1.0 / (2.0 * jnp.sqrt(squared + wave_floor)) / math.sqrt(full_rows * full_cols)
 
     place = jnp.stack([odd, row_at.astype(jnp.int32)])
+    kinds = 3 + substeps
+    flat, side, band = kernel_call(
+        functools.partial(inner_kernel, substeps),
+        (
+            shape((tiles, SUBLANES * segment(rows), LANES), f32),
+            shape((kinds, rows, LANES), f32),
+            shape((kinds, tiles, 4 * depth, LANES), f32),
+        ),
+        scratch=[
+            pltpu.VMEM((kinds, tiles, SUBLANES * segment(rows), LANES), f32),
+            pltpu.VMEM((tiles, segment(rows) + 4, SUBLANES, LANES), f32),
+            pltpu.VMEM((tiles, segment(rows) + 4, SUBLANES, LANES), f32),
+        ],
+        resident=(-1, -2, -3),
+    )((), height, rigidity, adhesion, forcing)
+    side_rows, band_rows = SUBLANES * segment(total), SUBLANES * segment(6 * depth)
+    side_shape = shape((kinds, side_rows, LANES), f32)
+    band_shape = shape((kinds, tiles + 1, band_rows, LANES), f32)
+    side, band = kernel_call(
+        functools.partial(edge_kernel, plan, substeps),
+        (side_shape, band_shape),
+        resident=(0, 1, -1, -2),
+    )((odd[None],), side, band, above, below, outer, inner)
     surface, *blocks = kernel_call(
-        functools.partial(evolve_kernel, plan, substeps),
+        functools.partial(outer_kernel, plan, substeps),
         tuple([shape((rows, cols), f32)] + [shape((share, rows), bf16)] * row_count),
         scratch=[
-            pltpu.VMEM((3 + substeps, tiles + 1, total, LANES), f32),
-            pltpu.VMEM((tiles + 1, seg + 4, SUBLANES, LANES), f32),
-            pltpu.VMEM((tiles + 1, seg + 4, SUBLANES, LANES), f32),
-            pltpu.VMEM((tiles, total, LANES), f32),
+            pltpu.VMEM(side_shape.shape, f32),
+            pltpu.VMEM(band_shape.shape, f32),
+            pltpu.VMEM((1, segment(total) + 4, SUBLANES, LANES), f32),
+            pltpu.VMEM((1, segment(total) + 4, SUBLANES, LANES), f32),
+            pltpu.VMEM((tiles + 1, segment(6 * depth) + 4, SUBLANES, LANES), f32),
+            pltpu.VMEM((tiles + 1, segment(6 * depth) + 4, SUBLANES, LANES), f32),
+            pltpu.VMEM((side_rows, LANES), f32),
+            pltpu.VMEM((tiles, band_rows, LANES), f32),
             pltpu.VMEM((cols, rows), bf16),
         ],
-    )((place,), height, rigidity, adhesion, forcing, above, below, outer, inner, outer_corner, inner_corner)
+        resident=(0, 1, 4),
+    )((place,), side, band, outer_corner, inner_corner, flat, height)
 
     def swap(pieces):
         return [pieces[0]] + [

time: 93.8 us -> 85.5 us (0.912)
  Pallas kernels: 46 us -> 42.1 us
  waiting for transfers between devices: 14.6 us -> 11.3 us
  local copies, waits for them, and re-layouts: 6.11 us -> 3.99 us
  starting transfers between devices: 16.7 us -> 17.8 us
    pallas_call x5 -> x7, Pallas kernels: 46 us -> 42.1 us  [run(): pl.pallas_call(body, out_shape=out_shape, in_specs=[pl.BlockSpec(memory_s...]
    ppermute x1, waiting for transfers between devices: 2.3 us -> 0.01 us  [on_device(): outer_corner = lax.ppermute(outer_corner, 'col', across)]
    slice x1 -> x0, local copies, waits for them, and re-layouts: 2.09 us -> none  [on_device(): forcing[:substeps - 1]]
    ppermute x1, starting transfers between devices: 0.68 us -> 2.43 us  [on_device(): outer = lax.ppermute(outer, 'col', across)]
    ppermute x1, starting transfers between devices: 3.05 us -> 1.58 us  [on_device(): above = lax.ppermute(down, 'row', ring_up)]
    ppermute x1, starting transfers between devices: 0.55 us -> 1.73 us  [on_device(): lax.ppermute(mine, 'col', [(i, (i - 2 * m) % col_count) for i in range(co...]
    ppermute x1, waiting for transfers between devices: 3.88 us -> 2.72 us  [on_device(): lax.ppermute(mine, 'col', [(i, (i - 2 * m) % col_count) for i in range(co...]
  transfers between devices with their start and end apart: 15 -> 15, of which waited for: 7 -> 7; matrix products, arithmetic and copies ran while one was open for 9% -> 10% of each run, Pallas kernels for 2% -> 26%
where the time goes in v2:
time: 85.5 us; the launch traced here: 85.1 us
  Pallas kernels  42.1 us (49%)
  starting transfers between devices  17.8 us (21%)
  waiting for transfers between devices  11.3 us (13%)
  other arithmetic  9.02 us (11%)
  local copies, waits for them, and re-layouts  3.99 us (5%)
  between operations  0.89 us (1%)
    pallas_call x7, Pallas kernels, run(): pl.pallas_call(body, out_shape=out_shape, in_specs=[pl.BlockSpec(memory_s...  42.1 us
    ppermute x6, starting transfers between devices, swap(): lax.ppermute(pieces[s], 'row', [(i, i ^ s) for i in range(row_count)])  8.77 us
    ppermute x6, waiting for transfers between devices, swap(): lax.ppermute(pieces[s], 'row', [(i, i ^ s) for i in range(row_count)])  7.92 us
    unnamed x28, local copies, waits for them, and re-layouts  3.87 us
    ppermute x1, waiting for transfers between devices, on_device(): lax.ppermute(mine, 'col', [(i, (i - 2 * m) % col_count) for i in range(co...  2.72 us
    ppermute x1, starting transfers between devices, on_device(): outer = lax.ppermute(outer, 'col', across)  2.43 us
    ppermute x1, starting transfers between devices, on_device(): below = lax.ppermute(up, 'row', ring_down)  2.25 us
    convert_element_type x1, other arithmetic, on_device(): table_re, table_im = (cos_y.astype(bf16), (-sin_y).astype(bf16))  1.97 us
  transfers between devices with their start and end apart: 15, of which 7 were waited for; matrix products, arithmetic and copies ran while one was open for 10% of the time, Pallas kernels for 26%

profile of v2, /device:TPU:0, one launch (start us, length us, event | category | flops | bytes accessed | tf_op | source)
XLA Modules:
  0.0 85.1 jit_solution(4547093515276381161)
XLA Ops:
  0.6 3.5 %shard_map.60 = (f32[64,256]{1,0:T(8,128)}, f32[64,256]{1,0:T(8,128)}, f32[256,128]{1,0:T(8,128)}, f32[256,128]{1,0:T(8,128)}) custom-call(s32[1]{0:T(128)} %bitcast.odd_ref, f32[512,256]{1,0:T(8,128)} %h_ref.5, f32[512,256]{1,0:T(8,128)} %g_ref.3, f32[512,256]{1,0:T(8,128)} %a_ref.3, bf16[4,512,256]{2,1,0:T(8,128)(2,1)} %f_ref.3), custom_call_target="tpu_custom_call" | custom-call | tf_op jit(solution)/shard_map/pallas_call | solution.py:437
  4.2 2.4 %collective-permute-start.2 = (f32[256,128]{1,0:T(8,128)}, f32[256,128]{1,0:T(8,128)S(1)}, u32[]{:S(2)}, u32[]{:S(2)}) collective-permute-start(f32[256,128]{1,0:T(8,128)} %get-tuple-element.26), channel_id=1, source_target_pairs={{0,3},{1,2},{2,1},{3,0},{4,7},{5,6},{6,5},{7,4},{8,11},{9,10},{10,... | collective-permute-start | bytes 393224 | tf_op jit(solution)/shard_map/ppermute | solution.py:487
  6.6 0.7 collective-permute-start.3
  7.3 1.6 %collective-permute-start = (f32[64,256]{1,0:T(8,128)}, f32[64,256]{1,0:T(8,128)S(1)}, u32[]{:S(2)}, u32[]{:S(2)}) collective-permute-start(f32[64,256]{1,0:T(8,128)} %get-tuple-element.24), channel_id=1, source_target_pairs={{0,4},{4,8},{8,12},{12,0},{1,5},{5,9},{9,13},{13,1},{2,6},{6,10},{... | collective-permute-start | bytes 196616 | tf_op jit(solution)/shard_map/ppermute | solution.py:485
  8.9 2.2 %collective-permute-start.1 = (f32[64,256]{1,0:T(8,128)}, f32[64,256]{1,0:T(8,128)S(1)}, u32[]{:S(2)}, u32[]{:S(2)}) collective-permute-start(f32[64,256]{1,0:T(8,128)} %get-tuple-element.25), channel_id=1, source_target_pairs={{0,12},{4,0},{8,4},{12,8},{1,13},{5,1},{9,5},{13,9},{2,14},{6,2},{... | collective-permute-start | bytes 196616 | tf_op jit(solution)/shard_map/ppermute | solution.py:486
  13.1 1.9 %add_convert_fusion = (bf16[16,32,1024]{2,1,0:T(8,128)(2,1)}, bf16[16,32,1024]{2,1,0:T(8,128)(2,1)}) fusion(f32[32,1024]{1,0:T(8,128)S(1)} %get-tuple-element.64, f32[16,1024]{1,0:T(8,128)S(1)} %get-tuple-element.53, f32[32,1024]{1,0:T(8,128)S(1)} %get-tuple-element.65, f32[16,1024]{1,0:T(8,128)S(1)} %get-tuple-element.52), kind=kLoop, calls=%fused_computation | loop fusion | flops 4194304 | bytes 2490368 | tf_op jit(solution)/shard_map/convert_element_type | solution.py:499
  16.2 1.6 %shard_map.62 = (f32[16,128]{1,0:T(8,128)}, f32[16,128]{1,0:T(8,128)}) custom-call(s32[1]{0:T(128)} %bitcast.odd_ref, f32[64,256]{1,0:T(8,128)} %copy-done.1, f32[64,256]{1,0:T(8,128)} %copy-done.2), custom_call_target="tpu_custom_call" | custom-call | tf_op jit(solution)/shard_map/pallas_call | solution.py:437
  18.8 15.8 %shard_map.59 = (f32[2,520,128]{2,1,0:T(8,128)}, f32[7,512,128]{2,1,0:T(8,128)}, f32[7,2,64,128]{3,2,1,0:T(8,128)}) custom-call(f32[512,256]{1,0:T(8,128)} %h_ref.5, f32[512,256]{1,0:T(8,128)} %g_ref.3, f32[512,256]{1,0:T(8,128)} %a_ref.3, bf16[4,512,256]{2,1,0:T(8,128)(2,1)} %f_ref.3), custom_call_target="tpu_custom_call" | custom-call | tf_op jit(solution)/shard_map/pallas_call | solution.py:437
  34.6 0.6 copy-done.6
  35.3 4.8 %shard_map.61 = (f32[7,552,128]{2,1,0:T(8,128)}, f32[7,3,104,128]{3,2,1,0:T(8,128)}) custom-call(s32[1]{0:T(128)} %bitcast.odd_ref, f32[7,512,128]{2,1,0:T(8,128)} %get-tuple-element.22.side_own_ref, f32[7,2,64,128]{3,2,1,0:T(8,128)} %get-tuple-element.23.band_own_ref, f32[64,256]{1,0:T(8,128)} %copy-done.1, f32[64,256]{1,0:T(8,128)} %copy-done.2, ...), custom_call_target="tpu_custom_call" | custom-call | tf_op jit(solution)/shard_map/pallas_call | solution.py:437
  40.8 9.8 %shard_map.63 = (f32[512,256]{1,0:T(8,128)}, bf16[64,512]{1,0:T(8,128)(2,1)}, bf16[64,512]{1,0:T(8,128)(2,1)}, bf16[64,512]{1,0:T(8,128)(2,1)}, bf16[64,512]{1,0:T(8,128)(2,1)}) custom-call(s32[2]{0:T(128)} %pad_add_fusion.1.place_ref, f32[7,552,128]{2,1,0:T(8,128)} %get-tuple-element.28.side_in_ref, f32[7,3,104,128]{3,2,1,0:T(8,128)} %get-tuple-element.29.band_in_ref, ...), custom_call_target="tpu_custom_call" | custom-call | tf_op jit(solution)/shard_map/pallas_call | solution.py:437
  50.5 2.6 %collective-permute-start.7 = (bf16[64,512]{1,0:T(8,128)(2,1)}, bf16[64,512]{1,0:T(8,128)(2,1)S(1)}, u32[]{:S(2)}, u32[]{:S(2)}) collective-permute-start(bf16[64,512]{1,0:T(8,128)(2,1)} %get-tuple-element.36), channel_id=1, source_target_pairs={{0,8},{4,12},{8,0},{12,4},{1,9},{5,13},{9,1},{13,5},{2,10},{6,14},... | collective-permute-start | bytes 196616 | tf_op jit(solution)/shard_map/ppermute | solution.py:572
  53.1 1.8 %collective-permute-start.8 = (bf16[64,512]{1,0:T(8,128)(2,1)}, bf16[64,512]{1,0:T(8,128)(2,1)S(1)}, u32[]{:S(2)}, u32[]{:S(2)}) collective-permute-start(bf16[64,512]{1,0:T(8,128)(2,1)} %get-tuple-element.37), channel_id=1, source_target_pairs={{0,12},{4,8},{8,4},{12,0},{1,13},{5,9},{9,5},{13,1},{2,14},{6,10},... | collective-permute-start | bytes 196616 | tf_op jit(solution)/shard_map/ppermute | solution.py:572
  54.9 1.0 %collective-permute-done.6.rest_1_ = bf16[64,512]{1,0:T(8,128)(2,1)S(1)} collective-permute-done((bf16[64,512]{1,0:T(8,128)(2,1)}, bf16[64,512]{1,0:T(8,128)(2,1)S(1)}, u32[]{:S(2)}, u32[]{:S(2)}) %collective-permute-start.6) | collective-permute-done | bytes 65568 | tf_op jit(solution)/shard_map/ppermute | solution.py:572
  55.9 2.9 %collective-permute-done.7.rest_2_ = bf16[64,512]{1,0:T(8,128)(2,1)S(1)} collective-permute-done((bf16[64,512]{1,0:T(8,128)(2,1)}, bf16[64,512]{1,0:T(8,128)(2,1)S(1)}, u32[]{:S(2)}, u32[]{:S(2)}) %collective-permute-start.7) | collective-permute-done | bytes 65568 | tf_op jit(solution)/shard_map/ppermute | solution.py:572
  58.8 0.7 collective-permute-done.8.rest_3_
  59.5 0.6 copy-done.10
  60.1 3.1 %shard_map.64 = (bf16[2,64,256]{2,1,0:T(8,128)(2,1)}, bf16[2,64,256]{2,1,0:T(8,128)(2,1)}, bf16[2,64,256]{2,1,0:T(8,128)(2,1)}, bf16[2,64,256]{2,1,0:T(8,128)(2,1)}) custom-call(s32[1]{0:T(128)} %bitcast.1.own_ref, f32[8,1024]{1,0:T(8,128)} %pad_maximum_fusion.1.phase_ref, bf16[512,1024]{1,0:T(8,128)(2,1)} %bitcast.14, bf16[512,1024]{1,0:T(8,128)(2,1)} %bitcast.13, ...), custom_call_target="tpu_custom_call" | custom-call | tf_op jit(solution)/shard_map/pallas_call | solution.py:437
  63.2 1.2 %collective-permute-start.9 = (bf16[2,64,256]{2,1,0:T(8,128)(2,1)}, bf16[2,64,256]{2,1,0:T(8,128)(2,1)S(1)}, u32[]{:S(2)}, u32[]{:S(2)}) collective-permute-start(bf16[2,64,256]{2,1,0:T(8,128)(2,1)} %get-tuple-element.39), channel_id=1, source_target_pairs={{0,4},{4,0},{8,12},{12,8},{1,5},{5,1},{9,13},{13,9},{2,6},{6,2},{1... | collective-permute-start | bytes 196616 | tf_op jit(solution)/shard_map/ppermute | solution.py:572
  64.4 1.2 %collective-permute-start.10 = (bf16[2,64,256]{2,1,0:T(8,128)(2,1)}, bf16[2,64,256]{2,1,0:T(8,128)(2,1)S(1)}, u32[]{:S(2)}, u32[]{:S(2)}) collective-permute-start(bf16[2,64,256]{2,1,0:T(8,128)(2,1)} %get-tuple-element.40), channel_id=1, source_target_pairs={{0,8},{4,12},{8,0},{12,4},{1,9},{5,13},{9,1},{13,5},{2,10},{6,14},... | collective-permute-start | bytes 196616 | tf_op jit(solution)/shard_map/ppermute | solution.py:572
  65.6 1.9 %collective-permute-start.11 = (bf16[2,64,256]{2,1,0:T(8,128)(2,1)}, bf16[2,64,256]{2,1,0:T(8,128)(2,1)S(1)}, u32[]{:S(2)}, u32[]{:S(2)}) collective-permute-start(bf16[2,64,256]{2,1,0:T(8,128)(2,1)} %get-tuple-element.41), channel_id=1, source_target_pairs={{0,12},{4,8},{8,4},{12,0},{1,13},{5,9},{9,5},{13,1},{2,14},{6,10},... | collective-permute-start | bytes 196616 | tf_op jit(solution)/shard_map/ppermute | solution.py:572
  67.6 1.1 %fusion.16 = (f32[16,2048]{1,0:T(8,128)S(1)}, f32[16,2048]{1,0:T(8,128)S(1)}, f32[16,2048]{1,0:T(8,128)S(1)}, f32[16,2048]{1,0:T(8,128)S(1)}) fusion(s32[2048]{0:T(1024)S(1)} %bitcast.21, s32[2048]{0:T(1024)S(1)} %pad_add_fusion, s32[16]{0:T(128)S(1)} %multiply_add_fusion), kind=kLoop, calls=%fused_computation.34 | loop fusion | flops 983040 | bytes 540736 | tf_op jit(solution)/shard_map/cos | solution.py:419
  68.7 2.2 %collective-permute-done.10 = bf16[2,64,256]{2,1,0:T(8,128)(2,1)S(1)} collective-permute-done((bf16[2,64,256]{2,1,0:T(8,128)(2,1)}, bf16[2,64,256]{2,1,0:T(8,128)(2,1)S(1)}, u32[]{:S(2)}, u32[]{:S(2)}) %collective-permute-start.10) | collective-permute-done | bytes 65568 | tf_op jit(solution)/shard_map/ppermute | solution.py:572
  70.8 1.2 %collective-permute-done.11 = bf16[2,64,256]{2,1,0:T(8,128)(2,1)S(1)} collective-permute-done((bf16[2,64,256]{2,1,0:T(8,128)(2,1)}, bf16[2,64,256]{2,1,0:T(8,128)(2,1)S(1)}, u32[]{:S(2)}, u32[]{:S(2)}) %collective-permute-start.11) | collective-permute-done | bytes 65568 | tf_op jit(solution)/shard_map/ppermute | solution.py:572
  72.0 0.9 %pad_maximum_fusion.rest_0_ = bf16[512,256]{1,0:T(8,128)(2,1)S(1)} fusion(bf16[128,256]{1,0:T(8,128)(2,1)S(1)} %bitcast.20, bf16[128,256]{1,0:T(8,128)(2,1)S(1)} %bitcast.19, bf16[128,256]{1,0:T(8,128)(2,1)S(1)} %bitcast.18, bf16[128,256]{1,0:T(8,128)(2,1)} %bitcast.17), kind=kLoop, calls=%fused_computation.4 | loop fusion | flops 1048576 | bytes 524288 | tf_op jit(solution)/shard_map/concatenate | solution.py:584
  72.9 1.7 %collective-permute-start.12 = (bf16[512,256]{1,0:T(8,128)(2,1)S(1)}, bf16[512,256]{1,0:T(8,128)(2,1)S(1)}, u32[]{:S(2)}, u32[]{:S(2)}) collective-permute-start(bf16[512,256]{1,0:T(8,128)(2,1)S(1)} %pad_maximum_fusion.rest_0_), channel_id=1, source_target_pairs={{0,2},{1,3},{2,0},{3,1},{4,6},{5,7},{6,4},{7,5},{8,10},{9,11},{10,... | collective-permute-start | bytes 786440 | tf_op jit(solution)/shard_map/ppermute | solution.py:586
  74.6 2.0 %negate_convert_fusion = (bf16[16,16,2048]{2,1,0:T(8,128)(2,1)}, bf16[16,16,2048]{2,1,0:T(8,128)(2,1)}) fusion(f32[16,2048]{1,0:T(8,128)S(1)} %get-tuple-element.50, f32[16,2048]{1,0:T(8,128)S(1)} %get-tuple-element.49, f32[16,2048]{1,0:T(8,128)S(1)} %get-tuple-element.51, f32[16,2048]{1,0:T(8,128)S(1)} %get-tuple-element.48), kind=kLoop, calls=%fused_computation.2 | loop fusion | flops 4718592 | bytes 2621440 | tf_op jit(solution)/shard_map/convert_element_type | solution.py:519
  76.6 2.7 %collective-permute-done.12.rest_1_ = bf16[512,256]{1,0:T(8,128)(2,1)S(1)} collective-permute-done((bf16[512,256]{1,0:T(8,128)(2,1)S(1)}, bf16[512,256]{1,0:T(8,128)(2,1)S(1)}, u32[]{:S(2)}, u32[]{:S(2)}) %collective-permute-start.12) | collective-permute-done | bytes 262176 | tf_op jit(solution)/shard_map/ppermute | solution.py:586
  79.3 0.9 %divide_multiply_fusion.mobility_ref = f32[256,256]{1,0:T(8,128)} fusion(f32[256]{0:T(256)S(1)} %get-tuple-element.59, f32[256]{0:T(256)S(1)} %get-tuple-element.58), kind=kLoop, calls=%fused_computation.5 | loop fusion | flops 327680 | bytes 264192 | tf_op jit(solution)/shard_map/div | solution.py:527
  80.2 0.6 collective-permute-done.14.rest_3_
  80.9 0.6 copy-done.5
  81.6 3.5 %shard_map.65 = f32[256,2,256]{2,1,0:T(2,128)} custom-call(bf16[256,2048]{1,0:T(8,128)(2,1)} %bitcast.16, bf16[256,2048]{1,0:T(8,128)(2,1)} %bitcast.15, f32[256,256]{1,0:T(8,128)} %divide_multiply_fusion.mobility_ref, bf16[512,256]{1,0:T(8,128)(2,1)} %copy-done, bf16[512,256]{1,0:T(8,128)(2,1)} %copy-done.3, bf16[512,256]{1,0:T(8,128)(2,1)} %copy-done.4, ...), custom_call_target="tpu_custom_call" | custom-call | tf_op jit(solution)/shard_map/pallas_call | solution.py:437
  (53 shorter events, 4.8 us)
Async XLA Ops:
  4.2 30.4 %collective-permute-start.2 = (f32[256,128]{1,0:T(8,128)}, f32[256,128]{1,0:T(8,128)S(1)}, u32[]{:S(2)}, u32[]{:S(2)}) collective-permute-start(f32[256,128]{1,0:T(8,128)} %get-tuple-element.26), channel_id=1, source_target_pairs={{0,3},{1,2},{2,1},{3,0},{4,7},{5,6},{6,5},{7,4},{8,11},{9,10},{10,... | collective-permute-start | bytes 393224 | tf_op jit(solution)/shard_map/ppermute | solution.py:487
  6.6 28.0 %collective-permute-start.3 = (f32[256,128]{1,0:T(8,128)}, f32[256,128]{1,0:T(8,128)S(1)}, u32[]{:S(2)}, u32[]{:S(2)}) collective-permute-start(f32[256,128]{1,0:T(8,128)} %get-tuple-element.27), channel_id=1, source_target_pairs={{0,1},{1,0},{2,3},{3,2},{4,5},{5,4},{6,7},{7,6},{8,9},{9,8},{10,11... | collective-permute-start | bytes 393224 | tf_op jit(solution)/shard_map/ppermute | solution.py:488
  7.3 7.7 %collective-permute-start = (f32[64,256]{1,0:T(8,128)}, f32[64,256]{1,0:T(8,128)S(1)}, u32[]{:S(2)}, u32[]{:S(2)}) collective-permute-start(f32[64,256]{1,0:T(8,128)} %get-tuple-element.24), channel_id=1, source_target_pairs={{0,4},{4,8},{8,12},{12,0},{1,5},{5,9},{9,13},{13,1},{2,6},{6,10},{... | collective-permute-start | bytes 196616 | tf_op jit(solution)/shard_map/ppermute | solution.py:485
  8.9 6.1 %collective-permute-start.1 = (f32[64,256]{1,0:T(8,128)}, f32[64,256]{1,0:T(8,128)S(1)}, u32[]{:S(2)}, u32[]{:S(2)}) collective-permute-start(f32[64,256]{1,0:T(8,128)} %get-tuple-element.25), channel_id=1, source_target_pairs={{0,12},{4,0},{8,4},{12,8},{1,13},{5,1},{9,5},{13,9},{2,14},{6,2},{... | collective-permute-start | bytes 196616 | tf_op jit(solution)/shard_map/ppermute | solution.py:486
  15.0 0.6 copy-start.1
  15.6 0.6 copy-start.2
  17.8 22.3 %collective-permute-start.4 = (f32[16,128]{1,0:T(8,128)}, f32[16,128]{1,0:T(8,128)S(1)}, u32[]{:S(2)}, u32[]{:S(2)}) collective-permute-start(f32[16,128]{1,0:T(8,128)} %get-tuple-element.30), channel_id=1, source_target_pairs={{0,3},{1,2},{2,1},{3,0},{4,7},{5,6},{6,5},{7,4},{8,11},{9,10},{10,... | collective-permute-start | bytes 24584 | tf_op jit(solution)/shard_map/ppermute | solution.py:492
  17.8 22.3 %collective-permute-start.5 = (f32[16,128]{1,0:T(8,128)}, f32[16,128]{1,0:T(8,128)S(1)}, u32[]{:S(2)}, u32[]{:S(2)}) collective-permute-start(f32[16,128]{1,0:T(8,128)} %get-tuple-element.31), channel_id=1, source_target_pairs={{0,1},{1,0},{2,3},{3,2},{4,5},{5,4},{6,7},{7,6},{8,9},{9,8},{10,11... | collective-permute-start | bytes 24584 | tf_op jit(solution)/shard_map/ppermute | solution.py:493
  34.6 0.7 copy-start.6
  34.6 0.7 copy-start.7
  40.1 0.6 copy-start.11
  40.2 0.6 copy-start.12
  50.5 5.4 %collective-permute-start.6 = (bf16[64,512]{1,0:T(8,128)(2,1)}, bf16[64,512]{1,0:T(8,128)(2,1)S(1)}, u32[]{:S(2)}, u32[]{:S(2)}) collective-permute-start(bf16[64,512]{1,0:T(8,128)(2,1)} %get-tuple-element.35), channel_id=1, source_target_pairs={{0,4},{4,0},{8,12},{12,8},{1,5},{5,1},{9,13},{13,9},{2,6},{6,2},{1... | collective-permute-start | bytes 196616 | tf_op jit(solution)/shard_map/ppermute | solution.py:572
  50.5 8.2 %collective-permute-start.7 = (bf16[64,512]{1,0:T(8,128)(2,1)}, bf16[64,512]{1,0:T(8,128)(2,1)S(1)}, u32[]{:S(2)}, u32[]{:S(2)}) collective-permute-start(bf16[64,512]{1,0:T(8,128)(2,1)} %get-tuple-element.36), channel_id=1, source_target_pairs={{0,8},{4,12},{8,0},{12,4},{1,9},{5,13},{9,1},{13,5},{2,10},{6,14},... | collective-permute-start | bytes 196616 | tf_op jit(solution)/shard_map/ppermute | solution.py:572
  53.1 6.4 %collective-permute-start.8 = (bf16[64,512]{1,0:T(8,128)(2,1)}, bf16[64,512]{1,0:T(8,128)(2,1)S(1)}, u32[]{:S(2)}, u32[]{:S(2)}) collective-permute-start(bf16[64,512]{1,0:T(8,128)(2,1)} %get-tuple-element.37), channel_id=1, source_target_pairs={{0,12},{4,8},{8,4},{12,0},{1,13},{5,9},{9,5},{13,1},{2,14},{6,10},... | collective-permute-start | bytes 196616 | tf_op jit(solution)/shard_map/ppermute | solution.py:572
  55.9 3.6 %copy-start.8 = (bf16[64,512]{1,0:T(8,128)(2,1)}, bf16[64,512]{1,0:T(8,128)(2,1)S(1)}, u32[]{:S(2)}) copy-start(bf16[64,512]{1,0:T(8,128)(2,1)S(1)} %collective-permute-done.6.rest_1_) | copy-start | bytes 196612
  58.8 0.7 copy-start.9
  59.5 0.6 copy-start.10
  63.2 5.5 %collective-permute-start.9 = (bf16[2,64,256]{2,1,0:T(8,128)(2,1)}, bf16[2,64,256]{2,1,0:T(8,128)(2,1)S(1)}, u32[]{:S(2)}, u32[]{:S(2)}) collective-permute-start(bf16[2,64,256]{2,1,0:T(8,128)(2,1)} %get-tuple-element.39), channel_id=1, source_target_pairs={{0,4},{4,0},{8,12},{12,8},{1,5},{5,1},{9,13},{13,9},{2,6},{6,2},{1... | collective-permute-start | bytes 196616 | tf_op jit(solution)/shard_map/ppermute | solution.py:572
  64.4 6.4 %collective-permute-start.10 = (bf16[2,64,256]{2,1,0:T(8,128)(2,1)}, bf16[2,64,256]{2,1,0:T(8,128)(2,1)S(1)}, u32[]{:S(2)}, u32[]{:S(2)}) collective-permute-start(bf16[2,64,256]{2,1,0:T(8,128)(2,1)} %get-tuple-element.40), channel_id=1, source_target_pairs={{0,8},{4,12},{8,0},{12,4},{1,9},{5,13},{9,1},{13,5},{2,10},{6,14},... | collective-permute-start | bytes 196616 | tf_op jit(solution)/shard_map/ppermute | solution.py:572
  65.6 6.4 %collective-permute-start.11 = (bf16[2,64,256]{2,1,0:T(8,128)(2,1)}, bf16[2,64,256]{2,1,0:T(8,128)(2,1)S(1)}, u32[]{:S(2)}, u32[]{:S(2)}) collective-permute-start(bf16[2,64,256]{2,1,0:T(8,128)(2,1)} %get-tuple-element.41), channel_id=1, source_target_pairs={{0,12},{4,8},{8,4},{12,0},{1,13},{5,9},{9,5},{13,1},{2,14},{6,10},... | collective-permute-start | bytes 196616 | tf_op jit(solution)/shard_map/ppermute | solution.py:572
  72.9 8.0 %copy-start = (bf16[512,256]{1,0:T(8,128)(2,1)}, bf16[512,256]{1,0:T(8,128)(2,1)S(1)}, u32[]{:S(2)}) copy-start(bf16[512,256]{1,0:T(8,128)(2,1)S(1)} %pad_maximum_fusion.rest_0_) | copy-start | bytes 786436
  72.9 6.4 %collective-permute-start.12 = (bf16[512,256]{1,0:T(8,128)(2,1)S(1)}, bf16[512,256]{1,0:T(8,128)(2,1)S(1)}, u32[]{:S(2)}, u32[]{:S(2)}) collective-permute-start(bf16[512,256]{1,0:T(8,128)(2,1)S(1)} %pad_maximum_fusion.rest_0_), channel_id=1, source_target_pairs={{0,2},{1,3},{2,0},{3,1},{4,6},{5,7},{6,4},{7,5},{8,10},{9,11},{10,... | collective-permute-start | bytes 786440 | tf_op jit(solution)/shard_map/ppermute | solution.py:586
  76.6 3.6 %collective-permute-start.13 = (bf16[512,256]{1,0:T(8,128)(2,1)S(1)}, bf16[512,256]{1,0:T(8,128)(2,1)S(1)}, u32[]{:S(2)}, u32[]{:S(2)}) collective-permute-start(bf16[512,256]{1,0:T(8,128)(2,1)S(1)} %pad_maximum_fusion.rest_0_), channel_id=1, source_target_pairs={{0,1},{1,0},{2,3},{3,2},{4,5},{5,4},{6,7},{7,6},{8,9},{9,8},{10,11... | collective-permute-start | bytes 786440 | tf_op jit(solution)/shard_map/ppermute | solution.py:589
  79.3 1.5 %copy-start.3 = (bf16[512,256]{1,0:T(8,128)(2,1)}, bf16[512,256]{1,0:T(8,128)(2,1)S(1)}, u32[]{:S(2)}) copy-start(bf16[512,256]{1,0:T(8,128)(2,1)S(1)} %collective-permute-done.12.rest_1_) | copy-start | bytes 786436
  79.3 1.5 %collective-permute-start.14 = (bf16[512,256]{1,0:T(8,128)(2,1)S(1)}, bf16[512,256]{1,0:T(8,128)(2,1)S(1)}, u32[]{:S(2)}, u32[]{:S(2)}) collective-permute-start(bf16[512,256]{1,0:T(8,128)(2,1)S(1)} %collective-permute-done.12.rest_1_), channel_id=1, source_target_pairs={{0,1},{1,0},{2,3},{3,2},{4,5},{5,4},{6,7},{7,6},{8,9},{9,8},{10,11... | collective-permute-start | bytes 786440 | tf_op jit(solution)/shard_map/ppermute | solution.py:589
  80.2 0.7 copy-start.4
  80.9 0.7 copy-start.5
